TPU v7x, 256 devices: a whole 4x4x8 slice. The times are simulated.
256 devices in a mesh: gx: 2 (over core), gy: 4 (over x), gz: 32 (over z, y).
Axes of the slice: x: 4, y: 4, z: 8, core: 2. Of those that a mesh axis runs over, the one named last changes fastest.
Arguments:
- a_blocks: bfloat16 [4, 8, 64, 64, 2048], P('gx', 'gy', 'gz'), may hold values from -0.15625 to 0.15625
- a_cols: int32 [4, 8, 64, 32], P('gx', 'gy', 'gz'), may hold values from 0 to 26, as said below
- a_count: int32 [4, 8, 64], P('gx', 'gy', 'gz'), may hold values from 14 to 27
- p_blocks: bfloat16 [4, 8, 64, 64, 512], P('gx', 'gy', 'gz'), may hold values from -0.75 to 0.75
- p_cols: int32 [4, 8, 64, 8], P('gx', 'gy', 'gz'), may hold values from 0 to 7, as said below
- p_count: int32 [4, 8, 64], P('gx', 'gy', 'gz'), may hold values from 1 to 8
- coarse_row: int32 [2, 4, 32], P('gx', 'gy', 'gz'), may hold values from 0 to 511, as said below
Outputs:
- coarse_matrix: bfloat16 [512, 64, 8192], P(('gx', 'gy', 'gz'))
Inputs may be any that keep to these rules, and one draw needn't show every extreme that they name: `a_cols`: in each row the first a_count entries are distinct. `p_cols`: each row holds 0 to 7 once each, 0 in slot 0. `coarse_row`: values are distinct. Row r belongs to device r // 2 in mesh order; aggregate (u, v, w) goes to a row of a device with gx = u and gy = v. A device gets at most 2 aggregates, and in each group of devices with equal gx and gy one device gets exactly 2.
All inputs are finite; a program needn't handle non-finite values.
Results may differ from a plain program's by a relative error of at most 0.005.
Values may be sent and summed in bfloat16 or wider, within the bound.
No kernel may reach another device: no remote copies, remote signals or barrier semaphores. Data moves between devices by JAX's collectives and lax.ppermute only.
A program may use at most 192 MiB of HBM per device.

v0:
```python
import jax
import jax.numpy as jnp
from jax import lax
from jax.sharding import PartitionSpec as P

CLASS_PICKS = ((0,), (1, 2), (3,))


def padded(shard, sides, width):
    for axis, dim in sides:
        peers, length = (lax.axis_size(axis), shard.shape[dim])
        up = [(i, (i + 1) % peers) for i in range(peers - 1)]
        down = [(j, i) for i, j in up]
        last = lax.slice_in_dim(shard, length - width, length, axis=dim)
        initial = lax.slice_in_dim(shard, 0, width, axis=dim)
        before = lax.ppermute(last, axis, up)
        after = lax.ppermute(initial, axis, down)
        shard = jnp.concatenate([before, shard, after], axis=dim)
    return shard


def split_code(code_list):
    return (code_list // 9 - 1, code_list // 3 % 3 - 1, code_list % 3 - 1)


def axis_slot(parity, offset, code_bit):
    landing = parity + offset
    shifted = jnp.floor_divide(landing, 2)
    facing = jnp.where(jnp.remainder(landing, 2) == 0, -1, 1)
    return shifted[:, None] + code_bit[None, :] * facing[:, None]


def slot_table(parity_x, parity_y, parity_z, code_list, live_count):
    offset_x, offset_y, offset_z = split_code(code_list)
    code_range = jnp.arange(8, dtype=jnp.int32)
    slot_x = axis_slot(parity_x, offset_x, code_range % 2)
    slot_y = axis_slot(parity_y, offset_y, code_range // 2 % 2)
    slot_z = axis_slot(parity_z, offset_z, code_range // 4)
    target = (slot_x + 1) * 9 + (slot_y + 1) * 3 + (slot_z + 1)
    live = jnp.arange(code_list.shape[0], dtype=jnp.int32) < live_count
    return (target[:, :, None] == jnp.arange(28, dtype=jnp.int32)[None, None, :]) & live[
        :, None, None
    ]


def place_rows(p_blocks, p_cols, p_count):
    shape_in = p_blocks.shape
    block_size = shape_in[3]
    blocks = p_blocks.reshape(shape_in[:3] + (block_size, 8, block_size))
    code_range = jnp.arange(8, dtype=jnp.int32)
    live = code_range < p_count[..., None]
    chooser = ((p_cols[..., None] == code_range) & live[..., None]).astype(jnp.bfloat16)
    placed = jnp.einsum("xyzqc,xyzfqb->xyzfcb", chooser, blocks, preferred_element_type=jnp.float32)
    return placed.astype(jnp.bfloat16).reshape(shape_in)


def extend(field):
    return padded(field, (("gx", 0), ("gy", 1), ("gz", 2)), 1)


def coarse_sum(wide_placed, wide_product, block_size):
    extent = wide_product.shape[:3]
    groups = tuple(((size_along - 2) // 2 for size_along in extent))
    total = jnp.zeros(groups + (block_size, 5, 5, 5, block_size), jnp.float32)
    for class_x in range(3):
        for class_y in range(3):
            for class_z in range(3):
                code = (class_x != 1) * 1 + (class_y != 1) * 2 + (class_z != 1) * 4
                partial_value = jnp.zeros(groups + (block_size, 28 * block_size), jnp.float32)
                for start_x in CLASS_PICKS[class_x]:
                    for start_y in CLASS_PICKS[class_y]:
                        for start_z in CLASS_PICKS[class_z]:
                            window = (
                                slice(start_x, start_x + 2 * groups[0] - 1, 2),
                                slice(start_y, start_y + 2 * groups[1] - 1, 2),
                                slice(start_z, start_z + 2 * groups[2] - 1, 2),
                            )
                            blocks_p = wide_placed[window][
                                ..., code * block_size : (code + 1) * block_size
                            ]
                            blocks_ap = wide_product[window]
                            partial_value = partial_value + jnp.einsum(
                                "uvwfa,uvwfe->uvwae",
                                blocks_p,
                                blocks_ap,
                                preferred_element_type=jnp.float32,
                            )
                partial_value = partial_value.reshape(groups + (block_size, 28, block_size))[
                    ..., :27, :
                ]
                partial_value = partial_value.reshape(groups + (block_size, 3, 3, 3, block_size))
                total = total.at[
                    :,
                    :,
                    :,
                    :,
                    class_x : class_x + 3,
                    class_y : class_y + 3,
                    class_z : class_z + 3,
                    :,
                ].add(partial_value)
    return total


def local(a_blocks, a_cols, a_count, p_blocks, p_cols, p_count, coarse_row):
    box_x, box_y, box_z, block_size = a_blocks.shape[:4]
    slot_count = a_cols.shape[3]
    row_count = box_x * box_y * box_z
    placed = place_rows(p_blocks, p_cols, p_count)
    wide_placed = extend(placed)
    flat_placed = wide_placed.reshape(-1, block_size, 8 * block_size)
    row_ids = jnp.arange(row_count, dtype=jnp.int32)
    local_x = row_ids // (box_y * box_z)
    local_y = row_ids // box_z % box_y
    local_z = row_ids % box_z

    def one_row(row_item):
        row_blocks, code_list, live_count, at_x, at_y, at_z = row_item
        offset_x, offset_y, offset_z = split_code(code_list)
        flat_index = ((at_x + offset_x + 1) * (box_y + 2) + (at_y + offset_y + 1)) * (box_z + 2) + (
            at_z + offset_z + 1
        )
        pieces = jnp.take(flat_placed, flat_index, axis=0).reshape(
            slot_count, block_size, 8, block_size
        )
        chooser = slot_table(at_x % 2, at_y % 2, at_z % 2, code_list, live_count)
        row_split = row_blocks.reshape(block_size, slot_count, block_size)
        partial_value = jnp.einsum(
            "akc,kcqb->kaqb", row_split, pieces, preferred_element_type=jnp.float32
        )
        summed = jnp.einsum(
            "kqe,kaqb->aeb",
            chooser.astype(jnp.float32),
            partial_value,
            precision=lax.Precision.HIGHEST,
        )
        return summed.reshape(block_size, 28 * block_size).astype(jnp.bfloat16)

    product = lax.map(
        one_row,
        (
            a_blocks.reshape(row_count, block_size, slot_count * block_size),
            a_cols.reshape(row_count, slot_count),
            a_count.reshape(row_count),
            local_x,
            local_y,
            local_z,
        ),
    )
    product = product.reshape(box_x, box_y, box_z, block_size, 28 * block_size)
    wide_product = extend(product)
    total = coarse_sum(wide_placed, wide_product, block_size)
    coarse_rows = total.reshape(-1, block_size, 125 * block_size)
    coarse_rows = jnp.pad(coarse_rows, ((0, 0), (0, 0), (0, 3 * block_size))).astype(jnp.bfloat16)
    aggregate_count = coarse_rows.shape[0]
    row_targets = coarse_row.reshape(aggregate_count)
    capacity = 2 * aggregate_count
    group_size = lax.axis_size("gz")
    group_base = (lax.axis_index("gx") * lax.axis_size("gy") + lax.axis_index("gy")) * group_size
    slot_base = (group_base + lax.axis_index("gz")) * capacity
    owner_local = row_targets // capacity - group_base
    owner_hits = owner_local[None, :] == jnp.arange(group_size, dtype=jnp.int32)[:, None]
    outgoing = jnp.where(
        owner_hits[:, :, None, None], coarse_rows[None], jnp.zeros((), jnp.bfloat16)
    )
    outgoing = outgoing.reshape(group_size * aggregate_count, block_size, 128 * block_size)
    outgoing_targets = jnp.where(owner_hits, row_targets[None, :], -1).reshape(
        group_size * aggregate_count
    )
    arrived_rows, arrived_targets = (
        lax.all_to_all(outgoing, "gz", split_axis=0, concat_axis=0, tiled=True),
        lax.all_to_all(outgoing_targets, "gz", split_axis=0, concat_axis=0, tiled=True),
    )
    matches = arrived_targets[:, None] == slot_base + jnp.arange(capacity, dtype=jnp.int32)[None, :]
    chosen = jnp.einsum(
        "nt,nab->tab",
        matches.astype(jnp.bfloat16),
        arrived_rows,
        preferred_element_type=jnp.float32,
    )
    return chosen.astype(jnp.bfloat16)


def solution(mesh):
    in_specs = (
        P("gx", "gy", "gz", None, None),
        P("gx", "gy", "gz", None),
        P("gx", "gy", "gz"),
        P("gx", "gy", "gz", None, None),
        P("gx", "gy", "gz", None),
        P("gx", "gy", "gz"),
        P("gx", "gy", "gz"),
    )
    out_specs = P(("gx", "gy", "gz"), None, None)
    return jax.shard_map(local, mesh=mesh, in_specs=in_specs, out_specs=out_specs, check_vma=False)
```

profile of v0, /device:TPU:122, one launch (start us, length us, event | category | flops | bytes accessed | tf_op | source)
XLA Modules:
  0.0 1491.7 jit_solution(13244560726575752994)
XLA Ops:
  15.5 9.9 collective-permute-done.2
  30.3 4.7 collective-permute-start.4
  38.2 10.3 all-to-all-start
  49.9 7.3 collective-permute-done.4
  57.2 7.4 collective-permute-done.5
  68.1 272.3 %while.40 = (s32[]{:T(128)}, bf16[8,64,1792]{2,1,0:T(8,128)(2,1)}, bf16[8,64,2048]{2,1,0:T(8,128)(2,1)}, s32[8]{0:T(128)S(1)}, s32[8,32]{1,0:T(8,128)}, /*index=...) while((s32[]{:T(128)}, bf16[8,64,1792]{2,1,0:T(8,128)(2,1)}, ...), condition=%wide.region_1.2_spmd, body=%wide.region_0.1_spmd.sunk | while | flops 487726656 | bytes 21342824 | solution.py:139
  93.0 7.9 fusion.152
  127.0 7.9 fusion.152
  161.0 7.9 fusion.152
  195.0 7.9 fusion.152
  229.0 7.9 fusion.152
  263.0 7.9 fusion.152
  296.9 7.9 fusion.152
  330.9 7.9 fusion.152
  345.7 4.1 collective-permute-start.6
  363.5 4.0 collective-permute-start.9
  384.9 18.0 %collective-permute-done.8 = bf16[4,1,2,64,1792]{4,3,2,1,0:T(8,128)(2,1)} collective-permute-done((bf16[4,1,2,64,1792]{4,3,2,1,0:T(8,128)(2,1)}, bf16[4,1,2,64,1792]{4,3,2,1,0:T(8,128)(2,1)}, u32[]{:S(2)}, u32[]{:S(2)}) %collective-permute-start.8) | collective-permute-done | bytes 1835040 | tf_op jit(solution)/shard_map/ppermute | solution.py:16
  445.7 7.4 collective-permute-start.10
  453.1 43.5 %collective-permute-done.11 = bf16[4,4,1,64,1792]{4,3,2,1,0:T(8,128)(2,1)} collective-permute-done((bf16[4,4,1,64,1792]{4,3,2,1,0:T(8,128)(2,1)}, bf16[4,4,1,64,1792]{4,3,2,1,0:T(8,128)(2,1)}, u32[]{:S(2)}, u32[]{:S(2)}) %collective-permute-start.11) | collective-permute-done | bytes 3670048 | tf_op jit(solution)/shard_map/ppermute | solution.py:17
  577.1 4.7 copy.214
  584.7 11.1 broadcast_select_fusion
  595.8 8.5 all-to-all-start.1
  605.0 809.0 %all-to-all-done.1 = bf16[32,64,8192]{2,1,0:T(8,128)(2,1)} async-done(((bf16[32,64,8192]{2,1,0:T(8,128)(2,1)}), bf16[32,64,8192]{2,1,0:T(8,128)(2,1)}, u32[]{:S(2)}, u32[]{:S(2)}) %all-to-all-start.1) | async-done | bytes 33554464 | tf_op jit(solution)/shard_map/all_to_all | solution.py:171
  1414.0 75.1 %fusion.40 = bf16[2,64,8192]{2,0,1:T(2,128)(2,1)S(1)} fusion(bf16[32,64,8192]{2,1,0:T(8,128)(2,1)} %all-to-all-done.1, s32[32]{0:T(128)S(1)} %reduce.54, s32[2]{0:T(128)S(1)} %iota_add_fusion), kind=kOutput, calls=%fused_computation.90 | convolution fusion | flops 68157504 | bytes 35651720 | tf_op jit(solution)/shard_map/nt,nab->tab/dot_general | solution.py:175
  (437 shorter events, 354.9 us)
Async XLA Ops:
  3.9 4.0 collective-permute-start
  6.0 3.4 collective-permute-start.1
  9.4 3.5 copy-start.27
  9.6 15.9 %collective-permute-start.2 = (bf16[4,1,2,64,512]{4,3,2,1,0:T(8,128)(2,1)S(1)}, bf16[4,1,2,64,512]{4,3,2,1,0:T(8,128)(2,1)S(1)}, u32[]{:S(2)}, u32[]{:S(2)}) collective-permute-start(bf16[4,1,2,64,512]{4,3,2,1,0:T(8,128)(2,1)S(1)} %get-tuple-element.581), channel_id=1, source_target_pairs={{0,32},{32,64},{64,96},{1,33},{33,65},{65,97},{2,34},{34,66},{66,9... | collective-permute-start | bytes 1572872 | tf_op jit(solution)/shard_map/ppermute | solution.py:16
  13.0 35.6 %copy-start.28 = (s32[2,2,2]{2,1,0:T(2,128)S(1)}, s32[2,2,2]{2,1,0:T(2,128)}, u32[]{:S(2)}) copy-start(s32[2,2,2]{2,1,0:T(2,128)} %param.65) | copy-start | bytes 100
  13.0 15.6 %collective-permute-start.3 = (bf16[4,1,2,64,512]{4,3,2,1,0:T(8,128)(2,1)S(1)}, bf16[4,1,2,64,512]{4,3,2,1,0:T(8,128)(2,1)S(1)}, u32[]{:S(2)}, u32[]{:S(2)}) collective-permute-start(bf16[4,1,2,64,512]{4,3,2,1,0:T(8,128)(2,1)S(1)} %get-tuple-element.582), channel_id=1, source_target_pairs={{32,0},{64,32},{96,64},{33,1},{65,33},{97,65},{34,2},{66,34},{98,6... | collective-permute-start | bytes 1572872 | tf_op jit(solution)/shard_map/ppermute | solution.py:17
  25.4 39.2 %copy-start.26 = (bf16[4,1,2,64,512]{4,3,2,1,0:T(8,128)(2,1)}, bf16[4,1,2,64,512]{4,3,2,1,0:T(8,128)(2,1)S(1)}, u32[]{:S(2)}) copy-start(bf16[4,1,2,64,512]{4,3,2,1,0:T(8,128)(2,1)S(1)} %collective-permute-done.2) | copy-start | bytes 1572868
  28.6 36.0 %copy-start.25 = (bf16[4,1,2,64,512]{4,3,2,1,0:T(8,128)(2,1)}, bf16[4,1,2,64,512]{4,3,2,1,0:T(8,128)(2,1)S(1)}, u32[]{:S(2)}) copy-start(bf16[4,1,2,64,512]{4,3,2,1,0:T(8,128)(2,1)S(1)} %collective-permute-done.3) | copy-start | bytes 1572868
  30.3 26.9 %collective-permute-start.4 = (bf16[4,4,1,64,512]{4,3,2,1,0:T(8,128)(2,1)}, bf16[4,4,1,64,512]{4,3,2,1,0:T(8,128)(2,1)}, u32[]{:S(2)}, u32[]{:S(2)}) collective-permute-start(bf16[4,4,1,64,512]{4,3,2,1,0:T(8,128)(2,1)} %get-tuple-element.577), channel_id=1, source_target_pairs={{0,1},{1,2},{2,3},{3,4},{4,5},{5,6},{6,7},{7,8},{8,9},{9,10},{10,1... | collective-permute-start | bytes 3145736 | tf_op jit(solution)/shard_map/ppermute | solution.py:16
  35.0 29.6 %collective-permute-start.5 = (bf16[4,4,1,64,512]{4,3,2,1,0:T(8,128)(2,1)}, bf16[4,4,1,64,512]{4,3,2,1,0:T(8,128)(2,1)}, u32[]{:S(2)}, u32[]{:S(2)}) collective-permute-start(bf16[4,4,1,64,512]{4,3,2,1,0:T(8,128)(2,1)} %get-tuple-element.578), channel_id=1, source_target_pairs={{1,0},{2,1},{3,2},{4,3},{5,4},{6,5},{7,6},{8,7},{9,8},{10,9},{11,1... | collective-permute-start | bytes 3145736 | tf_op jit(solution)/shard_map/ppermute | solution.py:17
  38.2 557.6 %all-to-all-start = ((s32[32,1,1]{2,1,0:T(1,128)}), s32[32,1,1]{2,1,0:T(1,128)S(1)}, u32[]{:S(2)}, u32[]{:S(2)}) async-start(s32[32,1,1]{2,1,0:T(1,128)} %compare_select_fusion.16), calls=%async_computation | async-start | bytes 32768 | tf_op jit(solution)/shard_map/all_to_all | solution.py:172
  340.4 3.0 copy-start
  344.4 12.3 collective-permute-start.7
  345.7 11.0 collective-permute-start.6
  360.4 42.5 %collective-permute-start.8 = (bf16[4,1,2,64,1792]{4,3,2,1,0:T(8,128)(2,1)}, bf16[4,1,2,64,1792]{4,3,2,1,0:T(8,128)(2,1)}, u32[]{:S(2)}, u32[]{:S(2)}) collective-permute-start(bf16[4,1,2,64,1792]{4,3,2,1,0:T(8,128)(2,1)} %get-tuple-element.575), channel_id=1, source_target_pairs={{0,32},{32,64},{64,96},{1,33},{33,65},{65,97},{2,34},{34,66},{66,9... | collective-permute-start | bytes 5505032 | tf_op jit(solution)/shard_map/ppermute | solution.py:16
  363.5 42.3 %collective-permute-start.9 = (bf16[4,1,2,64,1792]{4,3,2,1,0:T(8,128)(2,1)}, bf16[4,1,2,64,1792]{4,3,2,1,0:T(8,128)(2,1)}, u32[]{:S(2)}, u32[]{:S(2)}) collective-permute-start(bf16[4,1,2,64,1792]{4,3,2,1,0:T(8,128)(2,1)} %get-tuple-element.576), channel_id=1, source_target_pairs={{32,0},{64,32},{96,64},{33,1},{65,33},{97,65},{34,2},{66,34},{98,6... | collective-permute-start | bytes 5505032 | tf_op jit(solution)/shard_map/ppermute | solution.py:17
  412.6 84.0 %collective-permute-start.11 = (bf16[4,4,1,64,1792]{4,3,2,1,0:T(8,128)(2,1)}, bf16[4,4,1,64,1792]{4,3,2,1,0:T(8,128)(2,1)}, u32[]{:S(2)}, u32[]{:S(2)}) collective-permute-start(bf16[4,4,1,64,1792]{4,3,2,1,0:T(8,128)(2,1)} %get-tuple-element.565), channel_id=1, source_target_pairs={{1,0},{2,1},{3,2},{4,3},{5,4},{6,5},{7,6},{8,7},{9,8},{10,9},{11,1... | collective-permute-start | bytes 11010056 | tf_op jit(solution)/shard_map/ppermute | solution.py:17
  445.7 85.3 %collective-permute-start.10 = (bf16[4,4,1,64,1792]{4,3,2,1,0:T(8,128)(2,1)}, bf16[4,4,1,64,1792]{4,3,2,1,0:T(8,128)(2,1)}, u32[]{:S(2)}, u32[]{:S(2)}) collective-permute-start(bf16[4,4,1,64,1792]{4,3,2,1,0:T(8,128)(2,1)} %get-tuple-element.566), channel_id=1, source_target_pairs={{0,1},{1,2},{2,3},{3,4},{4,5},{5,6},{6,7},{7,8},{8,9},{9,10},{10,1... | collective-permute-start | bytes 11010056 | tf_op jit(solution)/shard_map/ppermute | solution.py:16
  499.6 4.3 copy-start.1
  506.5 6.1 copy-start.3
  534.0 4.4 copy-start.4
  565.4 2.9 slice-start.4
  565.7 2.9 copy-start.16
  595.8 818.2 %all-to-all-start.1 = ((bf16[32,64,8192]{2,1,0:T(8,128)(2,1)}), bf16[32,64,8192]{2,1,0:T(8,128)(2,1)}, u32[]{:S(2)}, u32[]{:S(2)}) async-start(bf16[32,64,8192]{2,1,0:T(8,128)(2,1)} %broadcast_select_fusion), calls=%async_computation.1 | async-start | bytes 67108864 | tf_op jit(solution)/shard_map/all_to_all | solution.py:171
  (25 other events, 33.9 us)
where the time goes:
time: 1500 us; the launch traced here: 1490 us
  waiting for transfers between devices  903 us (60%)
  matrix products  240 us (16%)
  local copies, waits for them, and re-layouts  173 us (12%)
  other arithmetic  72.3 us (5%)
  starting transfers between devices  56 us (4%)
  loops' own time  46.3 us (3%)
    all_to_all x1, waiting for transfers between devices, local(): lax.all_to_all(outgoing, 'gz', split_axis=0, concat_axis=0, tiled=True)  809 us
    dot_general x1, matrix products, local(): jnp.einsum('nt,nab->tab', matches.astype(jnp.bfloat16), arrived_rows, pre...  75.1 us
    dot_general x64, matrix products, coarse_sum(): jnp.einsum('uvwfa,uvwfe->uvwae', blocks_p, blocks_ap, preferred_element_t...  72.2 us
    dot_general x8, matrix products, one_row(): jnp.einsum('kqe,kaqb->aeb', chooser.astype(jnp.float32), partial_value, p...  63.5 us
    ppermute x6, waiting for transfers between devices, padded(): after = lax.ppermute(initial, axis, down)  58.3 us
    gather x16, local copies, waits for them, and re-layouts, one_row(): jnp.take(flat_placed, flat_index, axis=0)  52.5 us
    another operation x1, loops' own time, local(): lax.map(one_row, (a_blocks.reshape(row_count, block_size, slot_count * bl...  46.3 us
    ppermute x6, waiting for transfers between devices, padded(): before = lax.ppermute(last, axis, up)  35.2 us
  transfers between devices with their start and end apart: 14, of which 9 were waited for; matrix products, arithmetic and copies ran while one was open for 26% of the time, Pallas kernels for 0%

commit v1 on v0

v1 whole, which is shorter than its diff:
```python
import jax
import jax.numpy as jnp
import numpy as np
from jax import lax
from jax.experimental import pallas as pl
from jax.experimental.pallas import tpu as pltpu
from jax.sharding import PartitionSpec as P

B = 64
REACH = (((-1, 0), (1,)), ((-1,), (0, 1)))
NAMED_BY = (((0, 0),), ((0, 1), (1, 0)), ((1, 1),))


def ring(axis):
    peers = lax.axis_size(axis)
    up = [(i, i + 1) for i in range(peers - 1)]
    return up, [(j, i) for i, j in up]


def extend(shard):
    for dim, axis in enumerate(("gx", "gy", "gz")):
        up, down = ring(axis)
        length = shard.shape[dim]
        before = lax.ppermute(lax.slice_in_dim(shard, length - 1, length, axis=dim), axis, up)
        after = lax.ppermute(lax.slice_in_dim(shard, 0, 1, axis=dim), axis, down)
        shard = jnp.concatenate([before, shard, after], axis=dim)
    return shard


def place_rows(p_blocks, p_cols, p_count):
    code_of = np.zeros((8, 8), np.int32)
    for row in range(8):
        parity = (row >> 2, (row >> 1) & 1, row & 1)
        for pos in range(8):
            bits = (pos >> 2, (pos >> 1) & 1, pos & 1)
            code_of[row, pos] = sum((b if s else 1 - b) << d for d, (b, s) in enumerate(zip(bits, parity)))
    blocks = p_blocks.reshape(8, B, 8 * B)
    slots = jnp.arange(8, dtype=jnp.int32)
    code = jnp.where(slots < p_count.reshape(8, 1), p_cols.reshape(8, 8), -1)
    code = jnp.repeat(code, B, axis=1)
    wanted = jnp.repeat(jnp.asarray(code_of), B, axis=1)
    lane = jnp.arange(8 * B, dtype=jnp.int32) % B
    pick = (code[:, :, None] == wanted[:, None, :]) & (lane[:, None] == lane[None, :])[None]
    placed = jnp.einsum(
        "rfk,rks->rfs", blocks, pick.astype(jnp.bfloat16), preferred_element_type=jnp.float32
    )
    return placed.astype(jnp.bfloat16).reshape(2, 2, 2, B, 8 * B)


def wide_index(x, y, z):
    return (x + 1) * 16 + (y + 1) * 4 + (z + 1)


def galerkin_kernel(cols, count, a_ref, wide_ref, low_ref, mid_ref, high_ref, slot_ref, left_ref, prod_ref):
    left_ref[...] = jnp.zeros(left_ref.shape, left_ref.dtype)
    for row in range(8):
        parity = (row >> 2, (row >> 1) & 1, row & 1)
        slot_ref[...] = jnp.zeros(slot_ref.shape, slot_ref.dtype)
        for k in range(27):
            at = jnp.where(k < count[row], cols[row, k], 27)
            slot_ref[at] = a_ref[row, :, k * B : (k + 1) * B]
        slabs = {}
        for gx in range(2):
            for gy in range(2):
                for gz in range(2):
                    near = [
                        (ox, oy, oz)
                        for ox in REACH[parity[0]][gx]
                        for oy in REACH[parity[1]][gy]
                        for oz in REACH[parity[2]][gz]
                    ]
                    a_side = jnp.concatenate(
                        [slot_ref[(ox + 1) * 9 + (oy + 1) * 3 + oz + 1] for ox, oy, oz in near], axis=1
                    )
                    p_side = jnp.concatenate(
                        [
                            wide_ref[wide_index(parity[0] + ox, parity[1] + oy, parity[2] + oz)]
                            for ox, oy, oz in near
                        ],
                        axis=0,
                    )
                    cube = jnp.dot(a_side, p_side, preferred_element_type=jnp.float32)
                    for px in range(2):
                        for py in range(2):
                            key = (gx + px, gy + py, gz)
                            piece = cube[:, (px * 2 + py) * 128 : (px * 2 + py + 1) * 128]
                            slabs[key] = slabs[key] + piece if key in slabs else piece
        gap = jnp.zeros((B, B), jnp.float32)
        for e0 in range(3):
            for e1 in range(3):
                slab = jnp.concatenate([slabs[e0, e1, 0], gap], axis=1) + jnp.concatenate(
                    [gap, slabs[e0, e1, 1]], axis=1
                )
                prod_ref[e0 * 3 + e1, row * B : (row + 1) * B, :] = slab.astype(jnp.bfloat16)
        turned = wide_ref[wide_index(*parity)].T
        for dx in range(3):
            for dy in range(3):
                for dz in range(3):
                    pos = 0
                    for d, s in zip((dx, dy, dz), parity):
                        hit = [p for q, p in NAMED_BY[d] if q == s]
                        pos = pos * 2 + hit[0] if hit and pos is not None else None
                        if pos is None:
                            break
                    if pos is None:
                        continue
                    first = (dz * 9 + dy * 3 + dx) * B
                    left_ref[first : first + B, row * B : (row + 1) * B] = turned[pos * B : (pos + 1) * B, :]
    for dz, out_ref in enumerate((low_ref, mid_ref, high_ref)):
        left = left_ref[dz * 9 * B : (dz + 1) * 9 * B, :]
        for m in range(9):
            part = jnp.dot(left, prod_ref[m], preferred_element_type=jnp.float32)
            out_ref[:, m] = part.astype(out_ref.dtype).reshape(9, B, 3 * B)


def contributions(a_blocks, a_cols, a_count, wide_placed, interpret=False):
    smem = pl.BlockSpec(memory_space=pltpu.SMEM)
    vmem = pl.BlockSpec(memory_space=pltpu.VMEM)
    return pl.pallas_call(
        galerkin_kernel,
        out_shape=[
            jax.ShapeDtypeStruct((9, 9, B, 3 * B), kind)
            for kind in (jnp.bfloat16, jnp.float32, jnp.bfloat16)
        ],
        in_specs=[smem, smem, vmem, vmem],
        out_specs=[vmem] * 3,
        scratch_shapes=[
            pltpu.VMEM((28, B, B), jnp.bfloat16),
            pltpu.VMEM((27 * B, 8 * B), jnp.bfloat16),
            pltpu.VMEM((9, 8 * B, 3 * B), jnp.bfloat16),
        ],
        interpret=interpret,
    )(a_cols.reshape(8, -1), a_count.reshape(8), a_blocks.reshape(8, B, -1), wide_placed.reshape(64, B, 8 * B))


def fold(low, mid, high, axis, dim, width):
    up, down = ring(axis)
    from_below = lax.ppermute(high.astype(jnp.bfloat16), axis, up)
    from_above = lax.ppermute(low.astype(jnp.bfloat16), axis, down)

    def spread(part, before, after):
        pads = [(0, 0, 0)] * part.ndim
        pads[dim] = (before * width, after * width, 0)
        return lax.pad(part.astype(jnp.float32), jnp.float32(0), pads)

    return spread(from_below, 0, 2) + spread(mid, 1, 1) + spread(from_above, 2, 0)


def local(a_blocks, a_cols, a_count, p_blocks, p_cols, p_count, coarse_row, interpret=False):
    group_size = lax.axis_size("gz")
    target = jnp.broadcast_to(coarse_row.reshape(1, 1), (group_size, 1))
    targets = lax.all_to_all(target, "gz", split_axis=0, concat_axis=0, tiled=True).reshape(group_size)

    wide_placed = extend(place_rows(p_blocks, p_cols, p_count))
    low, mid, high = contributions(a_blocks, a_cols, a_count, wide_placed, interpret)
    part = fold(low, mid, high, "gz", 3, B).reshape(3, 3, 3, 3, B, 5 * B)
    part = fold(part[0], part[1], part[2], "gy", 2, 1)
    part = fold(part[0], part[1], part[2], "gx", 0, 1).astype(jnp.bfloat16)
    coarse = part.reshape(25, B, 5 * B).transpose(1, 0, 2).reshape(B, 125 * B)
    coarse = jnp.pad(coarse, ((0, 0), (0, 3 * B)))

    width = 128 * B // group_size
    spread = coarse.reshape(B, group_size, width).transpose(1, 0, 2)
    pieces = lax.all_to_all(spread, "gz", split_axis=0, concat_axis=0, tiled=True)
    group = lax.axis_index("gx") * lax.axis_size("gy") + lax.axis_index("gy")
    slots = group * (2 * group_size) + jnp.arange(2 * group_size, dtype=jnp.int32)
    matches = slots[:, None] == targets[None, :]
    source = jnp.argmax(matches, axis=1).astype(jnp.int32)
    taken = jnp.any(matches, axis=1)
    sent = jnp.take(pieces, source, axis=0, mode="clip")
    sent = jnp.where(taken[:, None, None], sent, jnp.zeros((), jnp.bfloat16))
    mine = lax.all_to_all(sent, "gz", split_axis=0, concat_axis=0, tiled=True)
    return mine.reshape(group_size, 2, B, width).transpose(1, 2, 0, 3).reshape(2, B, 128 * B)


def solution(mesh):
    in_specs = (
        P("gx", "gy", "gz", None, None),
        P("gx", "gy", "gz", None),
        P("gx", "gy", "gz"),
        P("gx", "gy", "gz", None, None),
        P("gx", "gy", "gz", None),
        P("gx", "gy", "gz"),
        P("gx", "gy", "gz"),
    )
    out_specs = P(("gx", "gy", "gz"), None, None)
    return jax.shard_map(local, mesh=mesh, in_specs=in_specs, out_specs=out_specs, check_vma=False)
```

time: 1500 us -> 301 us (0.20)
  the two profiles are of different devices: /device:TPU:122 before, /device:TPU:8 now
where the time goes in v1:
time: 301 us; the launch traced here: 300 us
  waiting for transfers between devices  155 us (51%)
  blocking collectives  55.5 us (18%)
  starting transfers between devices  48.4 us (16%)
  other arithmetic  14.3 us (5%)
  Pallas kernels  12.2 us (4%)
  local copies, waits for them, and re-layouts  11.9 us (4%)
    ppermute x3, waiting for transfers between devices, fold(): from_below = lax.ppermute(high.astype(jnp.bfloat16), axis, up)  76.9 us
    all_to_all x1, blocking collectives, local(): mine = lax.all_to_all(sent, 'gz', split_axis=0, concat_axis=0, tiled=True)  55.5 us
    ppermute x3, waiting for transfers between devices, extend(): lax.ppermute(lax.slice_in_dim(shard, length - 1, length, axis=dim), axis,...  28.9 us
    all_to_all x1, waiting for transfers between devices, local(): lax.all_to_all(spread, 'gz', split_axis=0, concat_axis=0, tiled=True)  27.4 us
    all_to_all x1, starting transfers between devices, local(): lax.all_to_all(target, 'gz', split_axis=0, concat_axis=0, tiled=True)  13.9 us
    pallas_call x1, Pallas kernels, contributions(): pl.pallas_call(galerkin_kernel, out_shape=[jax.ShapeDtypeStruct((9, 9, B,...  12.2 us
    ppermute x3, waiting for transfers between devices, extend(): after = lax.ppermute(lax.slice_in_dim(shard, 0, 1, axis=dim), axis, down)  9.27 us
    ppermute x3, waiting for transfers between devices, fold(): from_above = lax.ppermute(low.astype(jnp.bfloat16), axis, down)  9.07 us
  transfers between devices with their start and end apart: 14, of which 11 were waited for; matrix products, arithmetic and copies ran while one was open for 3% of the time, Pallas kernels for 0%

profile of v1, /device:TPU:8, one launch (start us, length us, event | category | flops | bytes accessed | tf_op | source)
XLA Modules:
  0.0 300.1 jit_solution(10651648359510871040)
XLA Ops:
  7.9 2.1 collective-permute-done.1
  10.2 3.4 %collective-permute-start.2 = (bf16[4,1,2,64,512]{4,3,2,1,0:T(8,128)(2,1)S(1)}, bf16[4,1,2,64,512]{4,3,2,1,0:T(8,128)(2,1)S(1)}, u32[]{:S(2)}, u32[]{:S(2)}) collective-permute-start(bf16[4,1,2,64,512]{4,3,2,1,0:T(8,128)(2,1)S(1)} %get-tuple-element.23), channel_id=1, source_target_pairs={{0,32},{32,64},{64,96},{1,33},{33,65},{65,97},{2,34},{34,66},{66,9... | collective-permute-start | bytes 1572872 | tf_op jit(solution)/shard_map/ppermute | solution.py:24
  14.9 10.1 %collective-permute-done.2 = bf16[4,1,2,64,512]{4,3,2,1,0:T(8,128)(2,1)S(1)} collective-permute-done((bf16[4,1,2,64,512]{4,3,2,1,0:T(8,128)(2,1)S(1)}, bf16[4,1,2,64,512]{4,3,2,1,0:T(8,128)(2,1)S(1)}, u32[]{:S(2)}, u32[]{:S(2)}) %collective-permute-start.2) | collective-permute-done | bytes 524320 | tf_op jit(solution)/shard_map/ppermute | solution.py:24
  25.1 4.1 %collective-permute-done.3 = bf16[4,1,2,64,512]{4,3,2,1,0:T(8,128)(2,1)S(1)} collective-permute-done((bf16[4,1,2,64,512]{4,3,2,1,0:T(8,128)(2,1)S(1)}, bf16[4,1,2,64,512]{4,3,2,1,0:T(8,128)(2,1)S(1)}, u32[]{:S(2)}, u32[]{:S(2)}) %collective-permute-start.3) | collective-permute-done | bytes 524320 | tf_op jit(solution)/shard_map/ppermute | solution.py:25
  30.6 3.5 %collective-permute-start.4 = (bf16[4,4,1,64,512]{4,3,2,1,0:T(8,128)(2,1)}, bf16[4,4,1,64,512]{4,3,2,1,0:T(8,128)(2,1)}, u32[]{:S(2)}, u32[]{:S(2)}) collective-permute-start(bf16[4,4,1,64,512]{4,3,2,1,0:T(8,128)(2,1)} %get-tuple-element.21), channel_id=1, source_target_pairs={{0,1},{1,2},{2,3},{3,4},{4,5},{5,6},{6,7},{7,8},{8,9},{9,10},{10,1... | collective-permute-start | bytes 3145736 | tf_op jit(solution)/shard_map/ppermute | solution.py:24
  34.1 3.4 %collective-permute-start.5 = (bf16[4,4,1,64,512]{4,3,2,1,0:T(8,128)(2,1)S(1)}, bf16[4,4,1,64,512]{4,3,2,1,0:T(8,128)(2,1)}, u32[]{:S(2)}, u32[]{:S(2)}) collective-permute-start(bf16[4,4,1,64,512]{4,3,2,1,0:T(8,128)(2,1)S(1)} %get-tuple-element.22), channel_id=1, source_target_pairs={{1,0},{2,1},{3,2},{4,3},{5,4},{6,5},{7,6},{8,7},{9,8},{10,9},{11,1... | collective-permute-start | bytes 3145736 | tf_op jit(solution)/shard_map/ppermute | solution.py:25
  38.2 18.7 %collective-permute-done.4 = bf16[4,4,1,64,512]{4,3,2,1,0:T(8,128)(2,1)} collective-permute-done((bf16[4,4,1,64,512]{4,3,2,1,0:T(8,128)(2,1)}, bf16[4,4,1,64,512]{4,3,2,1,0:T(8,128)(2,1)}, u32[]{:S(2)}, u32[]{:S(2)}) %collective-permute-start.4) | collective-permute-done | bytes 1048608 | tf_op jit(solution)/shard_map/ppermute | solution.py:24
  56.9 3.0 %collective-permute-done.5 = bf16[4,4,1,64,512]{4,3,2,1,0:T(8,128)(2,1)} collective-permute-done((bf16[4,4,1,64,512]{4,3,2,1,0:T(8,128)(2,1)S(1)}, bf16[4,4,1,64,512]{4,3,2,1,0:T(8,128)(2,1)}, u32[]{:S(2)}, u32[]{:S(2)}) %collective-permute-start.5) | collective-permute-done | bytes 1048608 | tf_op jit(solution)/shard_map/ppermute | solution.py:25
  59.9 3.6 %pad_maximum_fusion = bf16[4,4,4,64,512]{4,3,2,1,0:T(8,128)(2,1)} fusion(bf16[4,4,1,64,512]{4,3,2,1,0:T(8,128)(2,1)} %collective-permute-done.5, bf16[4,1,2,64,512]{4,3,2,1,0:T(8,128)(2,1)S(1)} %collective-permute-done.3, bf16[1,2,2,64,512]{4,3,2,1,0:T(8,128)(2,1)S(1)} %collective-permute-done.1, bf16[2,2,2,64,512]{4,3,2,1,0:T(8,128)(2,1)S(1)} %bitcast.44, ...), kind=kLoop, calls=%fused_computation.6 | loop fusion | flops 12582912 | bytes 8388608 | tf_op jit(solution)/shard_map/concatenate | solution.py:26
  63.5 12.2 %shard_map.82 = (bf16[9,9,64,192]{3,2,1,0:T(8,128)(2,1)}, f32[9,9,64,192]{3,2,1,0:T(8,128)}, bf16[9,9,64,192]{3,2,1,0:T(8,128)(2,1)}) custom-call(s32[8,32]{1,0:T(8,128)} %bitcast.53, s32[8]{0:T(128)} %reshape.112.count, bf16[8,64,2048]{2,1,0:T(8,128)(2,1)} %bitcast.47, bf16[64,64,512]{2,1,0:T(8,128)(2,1)} %bitcast.38), custom_call_target="tpu_custom_call" | custom-call | tf_op jit(solution)/shard_map/pallas_call | solution.py:119
  75.7 3.2 %collective-permute-start.6 = (bf16[9,9,64,192]{3,2,1,0:T(8,128)(2,1)}, bf16[9,9,64,192]{3,2,1,0:T(8,128)(2,1)S(1)}, u32[]{:S(2)}, u32[]{:S(2)}) collective-permute-start(bf16[9,9,64,192]{3,2,1,0:T(8,128)(2,1)} %get-tuple-element.9), channel_id=1, source_target_pairs={{0,1},{1,2},{2,3},{3,4},{4,5},{5,6},{6,7},{7,8},{8,9},{9,10},{10,1... | collective-permute-start | bytes 5971976 | tf_op jit(solution)/shard_map/ppermute | solution.py:138
  78.9 2.8 collective-permute-start.7
  81.7 53.3 %collective-permute-done.6 = bf16[9,9,64,192]{3,2,1,0:T(8,128)(2,1)S(1)} collective-permute-done((bf16[9,9,64,192]{3,2,1,0:T(8,128)(2,1)}, bf16[9,9,64,192]{3,2,1,0:T(8,128)(2,1)S(1)}, u32[]{:S(2)}, u32[]{:S(2)}) %collective-permute-start.6) | collective-permute-done | bytes 1990688 | tf_op jit(solution)/shard_map/ppermute | solution.py:138
  135.0 4.9 %collective-permute-done.7 = bf16[9,9,64,192]{3,2,1,0:T(8,128)(2,1)S(1)} collective-permute-done((bf16[9,9,64,192]{3,2,1,0:T(8,128)(2,1)}, bf16[9,9,64,192]{3,2,1,0:T(8,128)(2,1)S(1)}, u32[]{:S(2)}, u32[]{:S(2)}) %collective-permute-start.7) | collective-permute-done | bytes 1990688 | tf_op jit(solution)/shard_map/ppermute | solution.py:139
  139.9 4.4 %fusion.14 = (bf16[9,9,64,320]{3,2,1,0:T(8,128)(2,1)S(1)}, f32[9,9,64,320]{3,2,1,0:T(8,128)S(1)}) fusion(bf16[9,9,64,192]{3,2,1,0:T(8,128)(2,1)S(1)} %collective-permute-done.7, f32[9,9,64,192]{3,2,1,0:T(8,128)} %get-tuple-element.10, bf16[9,9,64,192]{3,2,1,0:T(8,128)(2,1)S(1)} %collective-permute-done.6), kind=kLoop, calls=%fused_computation.32 | loop fusion | flops 8294400 | bytes 17915904 | tf_op jit(solution)/shard_map/convert.15
  144.6 3.4 %collective-permute-start.8 = (bf16[3,3,3,64,320]{4,3,2,1,0:T(8,128)(2,1)S(1)}, bf16[3,3,3,64,320]{4,3,2,1,0:T(8,128)(2,1)S(1)}, u32[]{:S(2)}, u32[]{:S(2)}) collective-permute-start(bf16[3,3,3,64,320]{4,3,2,1,0:T(8,128)(2,1)S(1)} %bitcast.49), channel_id=1, source_target_pairs={{0,32},{32,64},{64,96},{1,33},{33,65},{65,97},{2,34},{34,66},{66,9... | collective-permute-start | bytes 3317768 | tf_op jit(solution)/shard_map/ppermute | solution.py:138
  149.8 23.5 %collective-permute-done.8 = bf16[3,3,3,64,320]{4,3,2,1,0:T(8,128)(2,1)S(1)} collective-permute-done((bf16[3,3,3,64,320]{4,3,2,1,0:T(8,128)(2,1)S(1)}, bf16[3,3,3,64,320]{4,3,2,1,0:T(8,128)(2,1)S(1)}, u32[]{:S(2)}, u32[]{:S(2)}) %collective-permute-start.8) | collective-permute-done | bytes 1105952 | tf_op jit(solution)/shard_map/ppermute | solution.py:138
  173.3 4.2 %collective-permute-done.9 = bf16[3,3,3,64,320]{4,3,2,1,0:T(8,128)(2,1)S(1)} collective-permute-done((bf16[3,3,3,64,320]{4,3,2,1,0:T(8,128)(2,1)S(1)}, bf16[3,3,3,64,320]{4,3,2,1,0:T(8,128)(2,1)S(1)}, u32[]{:S(2)}, u32[]{:S(2)}) %collective-permute-start.9) | collective-permute-done | bytes 1105952 | tf_op jit(solution)/shard_map/ppermute | solution.py:139
  177.5 2.9 fusion.13
  184.5 13.9 %all-to-all-start = ((s32[32,1,1]{2,1,0:T(1,128)}), s32[32,1,1]{2,1,0:T(1,128)S(1)}, u32[]{:S(2)}, u32[]{:S(2)}) async-start(s32[32,1,1]{2,1,0:T(1,128)} %broadcast_in_dim.40), calls=%async_computation | async-start | bytes 32768 | tf_op jit(solution)/shard_map/all_to_all | solution.py:152
  203.5 3.4 %all-to-all-done = s32[32,1,1]{2,1,0:T(1,128)S(1)} async-done(((s32[32,1,1]{2,1,0:T(1,128)}), s32[32,1,1]{2,1,0:T(1,128)S(1)}, u32[]{:S(2)}, u32[]{:S(2)}) %all-to-all-start) | async-done | bytes 160 | tf_op jit(solution)/shard_map/all_to_all | solution.py:152
  206.9 6.4 %all-to-all-start.1 = ((bf16[32,64,256]{2,1,0:T(8,128)(2,1)}), bf16[32,64,256]{2,1,0:T(8,128)(2,1)S(1)}, u32[]{:S(2)}, u32[]{:S(2)}) async-start(bf16[32,64,256]{2,1,0:T(8,128)(2,1)} %bitcast.35), calls=%async_computation.1 | async-start | bytes 2097152 | tf_op jit(solution)/shard_map/all_to_all | solution.py:164
  214.7 27.4 %all-to-all-done.1 = bf16[32,64,256]{2,1,0:T(8,128)(2,1)S(1)} async-done(((bf16[32,64,256]{2,1,0:T(8,128)(2,1)}), bf16[32,64,256]{2,1,0:T(8,128)(2,1)S(1)}, u32[]{:S(2)}, u32[]{:S(2)}) %all-to-all-start.1) | async-done | bytes 1048608 | tf_op jit(solution)/shard_map/all_to_all | solution.py:164
  243.1 55.5 %all_to_all.16 = bf16[64,64,256]{2,1,0:T(8,128)(2,1)S(1)} all-to-all(bf16[64,64,256]{2,1,0:T(8,128)(2,1)S(1)} %broadcast_select_fusion), channel_id=1, replica_groups=mesh['gx'=2,'gy'=4,'gz'=32] {'gz'}, dimensions={0} | all-to-all | bytes 4194304 | tf_op jit(solution)/shard_map/all_to_all | solution.py:172
  (48 shorter events, 25.7 us)
Async XLA Ops:
  0.0 2.7 copy-start
  4.8 3.1 %collective-permute-start = (bf16[1,2,2,64,512]{4,3,2,1,0:T(8,128)(2,1)S(1)}, bf16[1,2,2,64,512]{4,3,2,1,0:T(8,128)(2,1)S(1)}, u32[]{:S(2)}, u32[]{:S(2)}) collective-permute-start(bf16[1,2,2,64,512]{4,3,2,1,0:T(8,128)(2,1)S(1)} %bitcast.51), channel_id=1, source_target_pairs={{0,128},{1,129},{2,130},{3,131},{4,132},{5,133},{6,134},{7,135},{8... | collective-permute-start | bytes 786440 | tf_op jit(solution)/shard_map/ppermute | solution.py:24
  6.6 3.4 %collective-permute-start.1 = (bf16[1,2,2,64,512]{4,3,2,1,0:T(8,128)(2,1)S(1)}, bf16[1,2,2,64,512]{4,3,2,1,0:T(8,128)(2,1)S(1)}, u32[]{:S(2)}, u32[]{:S(2)}) collective-permute-start(bf16[1,2,2,64,512]{4,3,2,1,0:T(8,128)(2,1)S(1)} %bitcast.50), channel_id=1, source_target_pairs={{128,0},{129,1},{130,2},{131,3},{132,4},{133,5},{134,6},{135,7},{1... | collective-permute-start | bytes 786440 | tf_op jit(solution)/shard_map/ppermute | solution.py:25
  10.2 14.9 %collective-permute-start.2 = (bf16[4,1,2,64,512]{4,3,2,1,0:T(8,128)(2,1)S(1)}, bf16[4,1,2,64,512]{4,3,2,1,0:T(8,128)(2,1)S(1)}, u32[]{:S(2)}, u32[]{:S(2)}) collective-permute-start(bf16[4,1,2,64,512]{4,3,2,1,0:T(8,128)(2,1)S(1)} %get-tuple-element.23), channel_id=1, source_target_pairs={{0,32},{32,64},{64,96},{1,33},{33,65},{65,97},{2,34},{34,66},{66,9... | collective-permute-start | bytes 1572872 | tf_op jit(solution)/shard_map/ppermute | solution.py:24
  13.6 15.6 %collective-permute-start.3 = (bf16[4,1,2,64,512]{4,3,2,1,0:T(8,128)(2,1)S(1)}, bf16[4,1,2,64,512]{4,3,2,1,0:T(8,128)(2,1)S(1)}, u32[]{:S(2)}, u32[]{:S(2)}) collective-permute-start(bf16[4,1,2,64,512]{4,3,2,1,0:T(8,128)(2,1)S(1)} %get-tuple-element.24), channel_id=1, source_target_pairs={{32,0},{64,32},{96,64},{33,1},{65,33},{97,65},{34,2},{66,34},{98,6... | collective-permute-start | bytes 1572872 | tf_op jit(solution)/shard_map/ppermute | solution.py:25
  29.5 8.0 %copy-start.2 = (s32[2,2,2]{2,1,0:T(2,128)S(1)}, s32[2,2,2]{2,1,0:T(2,128)}, u32[]{:S(2)}) copy-start(s32[2,2,2]{2,1,0:T(2,128)} %param.10) | copy-start | bytes 100
  30.6 26.2 %collective-permute-start.4 = (bf16[4,4,1,64,512]{4,3,2,1,0:T(8,128)(2,1)}, bf16[4,4,1,64,512]{4,3,2,1,0:T(8,128)(2,1)}, u32[]{:S(2)}, u32[]{:S(2)}) collective-permute-start(bf16[4,4,1,64,512]{4,3,2,1,0:T(8,128)(2,1)} %get-tuple-element.21), channel_id=1, source_target_pairs={{0,1},{1,2},{2,3},{3,4},{4,5},{5,6},{6,7},{7,8},{8,9},{9,10},{10,1... | collective-permute-start | bytes 3145736 | tf_op jit(solution)/shard_map/ppermute | solution.py:24
  34.1 25.8 %collective-permute-start.5 = (bf16[4,4,1,64,512]{4,3,2,1,0:T(8,128)(2,1)S(1)}, bf16[4,4,1,64,512]{4,3,2,1,0:T(8,128)(2,1)}, u32[]{:S(2)}, u32[]{:S(2)}) collective-permute-start(bf16[4,4,1,64,512]{4,3,2,1,0:T(8,128)(2,1)S(1)} %get-tuple-element.22), channel_id=1, source_target_pairs={{1,0},{2,1},{3,2},{4,3},{5,4},{6,5},{7,6},{8,7},{9,8},{10,9},{11,1... | collective-permute-start | bytes 3145736 | tf_op jit(solution)/shard_map/ppermute | solution.py:25
  75.7 59.4 %collective-permute-start.6 = (bf16[9,9,64,192]{3,2,1,0:T(8,128)(2,1)}, bf16[9,9,64,192]{3,2,1,0:T(8,128)(2,1)S(1)}, u32[]{:S(2)}, u32[]{:S(2)}) collective-permute-start(bf16[9,9,64,192]{3,2,1,0:T(8,128)(2,1)} %get-tuple-element.9), channel_id=1, source_target_pairs={{0,1},{1,2},{2,3},{3,4},{4,5},{5,6},{6,7},{7,8},{8,9},{9,10},{10,1... | collective-permute-start | bytes 5971976 | tf_op jit(solution)/shard_map/ppermute | solution.py:138
  78.9 61.0 %collective-permute-start.7 = (bf16[9,9,64,192]{3,2,1,0:T(8,128)(2,1)}, bf16[9,9,64,192]{3,2,1,0:T(8,128)(2,1)S(1)}, u32[]{:S(2)}, u32[]{:S(2)}) collective-permute-start(bf16[9,9,64,192]{3,2,1,0:T(8,128)(2,1)} %get-tuple-element.11), channel_id=1, source_target_pairs={{1,0},{2,1},{3,2},{4,3},{5,4},{6,5},{7,6},{8,7},{9,8},{10,9},{11,1... | collective-permute-start | bytes 5971976 | tf_op jit(solution)/shard_map/ppermute | solution.py:139
  144.6 28.8 %collective-permute-start.8 = (bf16[3,3,3,64,320]{4,3,2,1,0:T(8,128)(2,1)S(1)}, bf16[3,3,3,64,320]{4,3,2,1,0:T(8,128)(2,1)S(1)}, u32[]{:S(2)}, u32[]{:S(2)}) collective-permute-start(bf16[3,3,3,64,320]{4,3,2,1,0:T(8,128)(2,1)S(1)} %bitcast.49), channel_id=1, source_target_pairs={{0,32},{32,64},{64,96},{1,33},{33,65},{65,97},{2,34},{34,66},{66,9... | collective-permute-start | bytes 3317768 | tf_op jit(solution)/shard_map/ppermute | solution.py:138
  148.0 29.5 %collective-permute-start.9 = (bf16[3,3,3,64,320]{4,3,2,1,0:T(8,128)(2,1)S(1)}, bf16[3,3,3,64,320]{4,3,2,1,0:T(8,128)(2,1)S(1)}, u32[]{:S(2)}, u32[]{:S(2)}) collective-permute-start(bf16[3,3,3,64,320]{4,3,2,1,0:T(8,128)(2,1)S(1)} %bitcast.48), channel_id=1, source_target_pairs={{32,0},{64,32},{96,64},{33,1},{65,33},{97,65},{34,2},{66,34},{98,6... | collective-permute-start | bytes 3317768 | tf_op jit(solution)/shard_map/ppermute | solution.py:139
  180.6 19.3 %collective-permute-start.10 = (bf16[3,5,64,320]{3,2,1,0:T(8,128)(2,1)S(1)}, bf16[3,5,64,320]{3,2,1,0:T(8,128)(2,1)S(1)}, u32[]{:S(2)}, u32[]{:S(2)}) collective-permute-start(bf16[3,5,64,320]{3,2,1,0:T(8,128)(2,1)S(1)} %get-tuple-element.19), channel_id=1, source_target_pairs={{0,128},{1,129},{2,130},{3,131},{4,132},{5,133},{6,134},{7,135},{8... | collective-permute-start | bytes 1843208 | tf_op jit(solution)/shard_map/ppermute | solution.py:138
  181.9 18.0 %collective-permute-start.11 = (bf16[3,5,64,320]{3,2,1,0:T(8,128)(2,1)S(1)}, bf16[3,5,64,320]{3,2,1,0:T(8,128)(2,1)S(1)}, u32[]{:S(2)}, u32[]{:S(2)}) collective-permute-start(bf16[3,5,64,320]{3,2,1,0:T(8,128)(2,1)S(1)} %get-tuple-element.20), channel_id=1, source_target_pairs={{128,0},{129,1},{130,2},{131,3},{132,4},{133,5},{134,6},{135,7},{1... | collective-permute-start | bytes 1843208 | tf_op jit(solution)/shard_map/ppermute | solution.py:139
  184.5 22.4 %all-to-all-start = ((s32[32,1,1]{2,1,0:T(1,128)}), s32[32,1,1]{2,1,0:T(1,128)S(1)}, u32[]{:S(2)}, u32[]{:S(2)}) async-start(s32[32,1,1]{2,1,0:T(1,128)} %broadcast_in_dim.40), calls=%async_computation | async-start | bytes 32768 | tf_op jit(solution)/shard_map/all_to_all | solution.py:152
  206.9 35.3 %all-to-all-start.1 = ((bf16[32,64,256]{2,1,0:T(8,128)(2,1)}), bf16[32,64,256]{2,1,0:T(8,128)(2,1)S(1)}, u32[]{:S(2)}, u32[]{:S(2)}) async-start(bf16[32,64,256]{2,1,0:T(8,128)(2,1)} %bitcast.35), calls=%async_computation.1 | async-start | bytes 2097152 | tf_op jit(solution)/shard_map/all_to_all | solution.py:164
  243.1 57.0 %copy-start.1 = (bf16[2,2,2,64,512]{4,3,2,1,0:T(8,128)(2,1)S(1)}, bf16[2,2,2,64,512]{4,3,2,1,0:T(8,128)(2,1)}, u32[]{:S(2)}) copy-start(bf16[2,2,2,64,512]{4,3,2,1,0:T(8,128)(2,1)} %param.11) | copy-start | bytes 1572868

commit v2 on v1

--- a/solution.py
+++ b/solution.py
@@ -18,7 +18,7 @@
 
 
 def extend(shard):
-    for dim, axis in enumerate(("gx", "gy", "gz")):
+    for dim, axis in ((2, "gz"), (1, "gy"), (0, "gx")):
         up, down = ring(axis)
         length = shard.shape[dim]
         before = lax.ppermute(lax.slice_in_dim(shard, length - 1, length, axis=dim), axis, up)
@@ -104,10 +104,10 @@
                             break
                     if pos is None:
                         continue
-                    first = (dz * 9 + dy * 3 + dx) * B
+                    first = (dx * 9 + dz * 3 + dy) * B
                     left_ref[first : first + B, row * B : (row + 1) * B] = turned[pos * B : (pos + 1) * B, :]
-    for dz, out_ref in enumerate((low_ref, mid_ref, high_ref)):
-        left = left_ref[dz * 9 * B : (dz + 1) * 9 * B, :]
+    for dx, out_ref in enumerate((low_ref, mid_ref, high_ref)):
+        left = left_ref[dx * 9 * B : (dx + 1) * 9 * B, :]
         for m in range(9):
             part = jnp.dot(left, prod_ref[m], preferred_element_type=jnp.float32)
             out_ref[:, m] = part.astype(out_ref.dtype).reshape(9, B, 3 * B)
@@ -152,10 +152,12 @@
     targets = lax.all_to_all(target, "gz", split_axis=0, concat_axis=0, tiled=True).reshape(group_size)
 
     wide_placed = extend(place_rows(p_blocks, p_cols, p_count))
+    wide_placed, targets = lax.optimization_barrier((wide_placed, targets))
     low, mid, high = contributions(a_blocks, a_cols, a_count, wide_placed, interpret)
-    part = fold(low, mid, high, "gz", 3, B).reshape(3, 3, 3, 3, B, 5 * B)
-    part = fold(part[0], part[1], part[2], "gy", 2, 1)
-    part = fold(part[0], part[1], part[2], "gx", 0, 1).astype(jnp.bfloat16)
+    low, mid, high = (x.reshape(9, 3, 3, B, 3 * B) for x in (low, mid, high))
+    part = fold(low, mid, high, "gx", 1, 1).reshape(3, 3, 5, 3, B, 3 * B)
+    part = fold(part[0], part[1], part[2], "gz", 4, B)
+    part = fold(part[0], part[1], part[2], "gy", 1, 1).astype(jnp.bfloat16)
     coarse = part.reshape(25, B, 5 * B).transpose(1, 0, 2).reshape(B, 125 * B)
     coarse = jnp.pad(coarse, ((0, 0), (0, 3 * B)))
 

time: 301 us -> 252 us (0.84)
  waiting for transfers between devices: 155 us -> 109 us
  starting transfers between devices: 48.4 us -> 51.5 us
    ppermute x3, waiting for transfers between devices: 76.9 us -> 46.5 us  [fold(): from_below = lax.ppermute(high.astype(jnp.bfloat16), axis, up)]
    ppermute x3, waiting for transfers between devices: 28.9 us -> 12.7 us  [extend(): lax.ppermute(lax.slice_in_dim(shard, length - 1, length, axis=dim), axis,...]
    all_to_all x1, waiting for transfers between devices: 3.36 us -> 7.87 us  [local(): lax.all_to_all(target, 'gz', split_axis=0, concat_axis=0, tiled=True)]
  transfers between devices with their start and end apart: 14 -> 14, of which waited for: 11 -> 12; matrix products, arithmetic and copies ran while one was open for 3% -> 1% of each run, Pallas kernels for 0% -> 0%
where the time goes in v2:
time: 252 us
  waiting for transfers between devices  109 us (43%)
  blocking collectives  53.5 us (21%)
  starting transfers between devices  51.5 us (20%)
  other arithmetic  12.3 us (5%)
  Pallas kernels  12.2 us (5%)
  local copies, waits for them, and re-layouts  10.5 us (4%)
    all_to_all x1, blocking collectives, local(): mine = lax.all_to_all(sent, 'gz', split_axis=0, concat_axis=0, tiled=True)  53.5 us
    ppermute x3, waiting for transfers between devices, fold(): from_below = lax.ppermute(high.astype(jnp.bfloat16), axis, up)  46.5 us
    all_to_all x1, waiting for transfers between devices, local(): lax.all_to_all(spread, 'gz', split_axis=0, concat_axis=0, tiled=True)  25.3 us
    all_to_all x1, starting transfers between devices, local(): lax.all_to_all(target, 'gz', split_axis=0, concat_axis=0, tiled=True)  13.5 us
    ppermute x3, waiting for transfers between devices, extend(): lax.ppermute(lax.slice_in_dim(shard, length - 1, length, axis=dim), axis,...  12.7 us
    pallas_call x1, Pallas kernels, contributions(): pl.pallas_call(galerkin_kernel, out_shape=[jax.ShapeDtypeStruct((9, 9, B,...  12.2 us
    ppermute x3, starting transfers between devices, extend(): lax.ppermute(lax.slice_in_dim(shard, length - 1, length, axis=dim), axis,...  9.22 us
    ppermute x3, waiting for transfers between devices, fold(): from_above = lax.ppermute(low.astype(jnp.bfloat16), axis, down)  9.02 us
  transfers between devices with their start and end apart: 14, of which 12 were waited for; matrix products, arithmetic and copies ran while one was open for 1% of the time, Pallas kernels for 0%

profile of v2, /device:TPU:8, one launch (start us, length us, event | category | flops | bytes accessed | tf_op | source)
XLA Modules:
  0.0 251.7 jit_solution(5476092965088425976)
XLA Ops:
  4.8 3.5 %collective-permute-start = (bf16[2,2,1,64,512]{4,3,2,1,0:T(8,128)(2,1)S(1)}, bf16[2,2,1,64,512]{4,3,2,1,0:T(8,128)(2,1)S(1)}, u32[]{:S(2)}, u32[]{:S(2)}) collective-permute-start(bf16[2,2,1,64,512]{4,3,2,1,0:T(8,128)(2,1)S(1)} %get-tuple-element.29), channel_id=1, source_target_pairs={{0,1},{1,2},{2,3},{3,4},{4,5},{5,6},{6,7},{7,8},{8,9},{9,10},{10,1... | collective-permute-start | bytes 786440 | tf_op jit(solution)/shard_map/ppermute | solution.py:24
  10.7 4.1 %collective-permute-done = bf16[2,2,1,64,512]{4,3,2,1,0:T(8,128)(2,1)S(1)} collective-permute-done((bf16[2,2,1,64,512]{4,3,2,1,0:T(8,128)(2,1)S(1)}, bf16[2,2,1,64,512]{4,3,2,1,0:T(8,128)(2,1)S(1)}, u32[]{:S(2)}, u32[]{:S(2)}) %collective-permute-start) | collective-permute-done | bytes 262176 | tf_op jit(solution)/shard_map/ppermute | solution.py:24
  14.7 3.2 %collective-permute-done.1 = bf16[2,2,1,64,512]{4,3,2,1,0:T(8,128)(2,1)S(1)} collective-permute-done((bf16[2,2,1,64,512]{4,3,2,1,0:T(8,128)(2,1)S(1)}, bf16[2,2,1,64,512]{4,3,2,1,0:T(8,128)(2,1)S(1)}, u32[]{:S(2)}, u32[]{:S(2)}) %collective-permute-start.1) | collective-permute-done | bytes 262176 | tf_op jit(solution)/shard_map/ppermute | solution.py:25
  18.2 3.4 %collective-permute-start.2 = (bf16[2,1,4,64,512]{4,3,2,1,0:T(8,128)(2,1)S(1)}, bf16[2,1,4,64,512]{4,3,2,1,0:T(8,128)(2,1)S(1)}, u32[]{:S(2)}, u32[]{:S(2)}) collective-permute-start(bf16[2,1,4,64,512]{4,3,2,1,0:T(8,128)(2,1)S(1)} %get-tuple-element.27), channel_id=1, source_target_pairs={{0,32},{32,64},{64,96},{1,33},{33,65},{65,97},{2,34},{34,66},{66,9... | collective-permute-start | bytes 1572872 | tf_op jit(solution)/shard_map/ppermute | solution.py:24
  22.9 8.6 %collective-permute-done.2 = bf16[2,1,4,64,512]{4,3,2,1,0:T(8,128)(2,1)S(1)} collective-permute-done((bf16[2,1,4,64,512]{4,3,2,1,0:T(8,128)(2,1)S(1)}, bf16[2,1,4,64,512]{4,3,2,1,0:T(8,128)(2,1)S(1)}, u32[]{:S(2)}, u32[]{:S(2)}) %collective-permute-start.2) | collective-permute-done | bytes 524320 | tf_op jit(solution)/shard_map/ppermute | solution.py:24
  31.5 4.1 %collective-permute-done.3 = bf16[2,1,4,64,512]{4,3,2,1,0:T(8,128)(2,1)S(1)} collective-permute-done((bf16[2,1,4,64,512]{4,3,2,1,0:T(8,128)(2,1)S(1)}, bf16[2,1,4,64,512]{4,3,2,1,0:T(8,128)(2,1)S(1)}, u32[]{:S(2)}, u32[]{:S(2)}) %collective-permute-start.3) | collective-permute-done | bytes 524320 | tf_op jit(solution)/shard_map/ppermute | solution.py:25
  41.9 13.5 %all-to-all-start = ((s32[32,1,1]{2,1,0:T(1,128)}), s32[32,1,1]{2,1,0:T(1,128)S(1)}, u32[]{:S(2)}, u32[]{:S(2)}) async-start(s32[32,1,1]{2,1,0:T(1,128)} %broadcast_in_dim.44), calls=%async_computation | async-start | bytes 32768 | tf_op jit(solution)/shard_map/all_to_all | solution.py:152
  56.1 7.9 %all-to-all-done = s32[32,1,1]{2,1,0:T(1,128)S(1)} async-done(((s32[32,1,1]{2,1,0:T(1,128)}), s32[32,1,1]{2,1,0:T(1,128)S(1)}, u32[]{:S(2)}, u32[]{:S(2)}) %all-to-all-start) | async-done | bytes 160 | tf_op jit(solution)/shard_map/all_to_all | solution.py:152
  64.7 3.6 %pad_maximum_fusion = bf16[4,4,4,64,512]{4,3,2,1,0:T(8,128)(2,1)} fusion(bf16[1,4,4,64,512]{4,3,2,1,0:T(8,128)(2,1)} %collective-permute-done.5, bf16[2,1,4,64,512]{4,3,2,1,0:T(8,128)(2,1)S(1)} %collective-permute-done.3, bf16[2,2,1,64,512]{4,3,2,1,0:T(8,128)(2,1)S(1)} %collective-permute-done.1, bf16[2,2,2,64,512]{4,3,2,1,0:T(8,128)(2,1)S(1)} %bitcast.41, ...), kind=kLoop, calls=%fused_computation.6 | loop fusion | flops 12582912 | bytes 8388608 | tf_op jit(solution)/shard_map/concatenate | solution.py:26
  68.3 12.2 %shard_map.82 = (bf16[9,9,64,192]{3,2,1,0:T(8,128)(2,1)}, f32[9,9,64,192]{3,2,1,0:T(8,128)}, bf16[9,9,64,192]{3,2,1,0:T(8,128)(2,1)}) custom-call(s32[8,32]{1,0:T(8,128)} %bitcast.47, s32[8]{0:T(128)} %reshape.124.count, bf16[8,64,2048]{2,1,0:T(8,128)(2,1)} %bitcast.45, bf16[64,64,512]{2,1,0:T(8,128)(2,1)} %bitcast.36), custom_call_target="tpu_custom_call" | custom-call | tf_op jit(solution)/shard_map/pallas_call | solution.py:119
  80.5 2.7 %collective-permute-start.6 = (bf16[9,3,3,64,192]{4,3,2,1,0:T(8,128)(2,1)}, bf16[9,3,3,64,192]{4,3,2,1,0:T(8,128)(2,1)S(1)}, u32[]{:S(2)}, u32[]{:S(2)}) collective-permute-start(bf16[9,3,3,64,192]{4,3,2,1,0:T(8,128)(2,1)} %bitcast.49), channel_id=1, source_target_pairs={{0,128},{1,129},{2,130},{3,131},{4,132},{5,133},{6,134},{7,135},{8... | collective-permute-start | bytes 5971976 | tf_op jit(solution)/shard_map/ppermute | solution.py:138
  84.5 3.3 %collective-permute-done.6 = bf16[9,3,3,64,192]{4,3,2,1,0:T(8,128)(2,1)S(1)} collective-permute-done((bf16[9,3,3,64,192]{4,3,2,1,0:T(8,128)(2,1)}, bf16[9,3,3,64,192]{4,3,2,1,0:T(8,128)(2,1)S(1)}, u32[]{:S(2)}, u32[]{:S(2)}) %collective-permute-start.6) | collective-permute-done | bytes 1990688 | tf_op jit(solution)/shard_map/ppermute | solution.py:138
  87.8 2.5 collective-permute-done.7
  90.3 4.0 %fusion.14 = (bf16[9,5,3,64,192]{4,3,2,1,0:T(8,128)(2,1)S(1)}, f32[9,5,3,64,192]{4,3,2,1,0:T(8,128)S(1)}) fusion(bf16[9,3,3,64,192]{4,3,2,1,0:T(8,128)(2,1)S(1)} %collective-permute-done.7, f32[9,3,3,64,192]{4,3,2,1,0:T(8,128)} %bitcast.42, bf16[9,3,3,64,192]{4,3,2,1,0:T(8,128)(2,1)S(1)} %collective-permute-done.6), kind=kLoop, calls=%fused_computation.32 | loop fusion | flops 8294400 | bytes 17915904 | tf_op jit(solution)/shard_map/convert.15
  94.5 2.7 %collective-permute-start.8 = (bf16[3,5,3,64,192]{4,3,2,1,0:T(8,128)(2,1)S(1)}, bf16[3,5,3,64,192]{4,3,2,1,0:T(8,128)(2,1)S(1)}, u32[]{:S(2)}, u32[]{:S(2)}) collective-permute-start(bf16[3,5,3,64,192]{4,3,2,1,0:T(8,128)(2,1)S(1)} %get-tuple-element.21), channel_id=1, source_target_pairs={{0,1},{1,2},{2,3},{3,4},{4,5},{5,6},{6,7},{7,8},{8,9},{9,10},{10,1... | collective-permute-start | bytes 3317768 | tf_op jit(solution)/shard_map/ppermute | solution.py:138
  97.2 3.4 %collective-permute-start.9 = (bf16[3,5,3,64,192]{4,3,2,1,0:T(8,128)(2,1)S(1)}, bf16[3,5,3,64,192]{4,3,2,1,0:T(8,128)(2,1)S(1)}, u32[]{:S(2)}, u32[]{:S(2)}) collective-permute-start(bf16[3,5,3,64,192]{4,3,2,1,0:T(8,128)(2,1)S(1)} %get-tuple-element.22), channel_id=1, source_target_pairs={{1,0},{2,1},{3,2},{4,3},{5,4},{6,5},{7,6},{8,7},{9,8},{10,9},{11,1... | collective-permute-start | bytes 3317768 | tf_op jit(solution)/shard_map/ppermute | solution.py:139
  101.0 29.8 %collective-permute-done.8 = bf16[3,5,3,64,192]{4,3,2,1,0:T(8,128)(2,1)S(1)} collective-permute-done((bf16[3,5,3,64,192]{4,3,2,1,0:T(8,128)(2,1)S(1)}, bf16[3,5,3,64,192]{4,3,2,1,0:T(8,128)(2,1)S(1)}, u32[]{:S(2)}, u32[]{:S(2)}) %collective-permute-start.8) | collective-permute-done | bytes 1105952 | tf_op jit(solution)/shard_map/ppermute | solution.py:138
  130.7 2.4 collective-permute-done.9
  134.6 3.4 %collective-permute-start.10 = (bf16[5,3,64,320]{3,2,1,0:T(8,128)(2,1)S(1)}, bf16[5,3,64,320]{3,2,1,0:T(8,128)(2,1)S(1)}, u32[]{:S(2)}, u32[]{:S(2)}) collective-permute-start(bf16[5,3,64,320]{3,2,1,0:T(8,128)(2,1)S(1)} %get-tuple-element.23), channel_id=1, source_target_pairs={{0,32},{32,64},{64,96},{1,33},{33,65},{65,97},{2,34},{34,66},{66,9... | collective-permute-start | bytes 1843208 | tf_op jit(solution)/shard_map/ppermute | solution.py:138
  139.5 13.4 %collective-permute-done.10 = bf16[5,3,64,320]{3,2,1,0:T(8,128)(2,1)S(1)} collective-permute-done((bf16[5,3,64,320]{3,2,1,0:T(8,128)(2,1)S(1)}, bf16[5,3,64,320]{3,2,1,0:T(8,128)(2,1)S(1)}, u32[]{:S(2)}, u32[]{:S(2)}) %collective-permute-start.10) | collective-permute-done | bytes 614432 | tf_op jit(solution)/shard_map/ppermute | solution.py:138
  152.9 4.2 %collective-permute-done.11 = bf16[5,3,64,320]{3,2,1,0:T(8,128)(2,1)S(1)} collective-permute-done((bf16[5,3,64,320]{3,2,1,0:T(8,128)(2,1)S(1)}, bf16[5,3,64,320]{3,2,1,0:T(8,128)(2,1)S(1)}, u32[]{:S(2)}, u32[]{:S(2)}) %collective-permute-start.11) | collective-permute-done | bytes 614432 | tf_op jit(solution)/shard_map/ppermute | solution.py:139
  160.6 9.0 %all-to-all-start.1 = ((bf16[32,64,256]{2,1,0:T(8,128)(2,1)}), bf16[32,64,256]{2,1,0:T(8,128)(2,1)S(1)}, u32[]{:S(2)}, u32[]{:S(2)}) async-start(bf16[32,64,256]{2,1,0:T(8,128)(2,1)} %bitcast.33), calls=%async_computation.1 | async-start | bytes 2097152 | tf_op jit(solution)/shard_map/all_to_all | solution.py:166
  170.4 25.3 %all-to-all-done.1 = bf16[32,64,256]{2,1,0:T(8,128)(2,1)S(1)} async-done(((bf16[32,64,256]{2,1,0:T(8,128)(2,1)}), bf16[32,64,256]{2,1,0:T(8,128)(2,1)S(1)}, u32[]{:S(2)}, u32[]{:S(2)}) %all-to-all-start.1) | async-done | bytes 1048608 | tf_op jit(solution)/shard_map/all_to_all | solution.py:166
  196.6 53.5 %all_to_all.16 = bf16[64,64,256]{2,1,0:T(8,128)(2,1)S(1)} all-to-all(bf16[64,64,256]{2,1,0:T(8,128)(2,1)S(1)} %broadcast_select_fusion), channel_id=1, replica_groups=mesh['gx'=2,'gy'=4,'gz'=32] {'gz'}, dimensions={0} | all-to-all | bytes 4194304 | tf_op jit(solution)/shard_map/all_to_all | solution.py:174
  (48 shorter events, 27.0 us)
Async XLA Ops:
  0.0 2.7 %copy-start = (bf16[2,2,2,64,512]{4,3,2,1,0:T(8,128)(2,1)S(1)}, bf16[2,2,2,64,512]{4,3,2,1,0:T(8,128)(2,1)}, u32[]{:S(2)}) copy-start(bf16[2,2,2,64,512]{4,3,2,1,0:T(8,128)(2,1)} %param.11) | copy-start | bytes 1572868
  4.8 9.9 %collective-permute-start = (bf16[2,2,1,64,512]{4,3,2,1,0:T(8,128)(2,1)S(1)}, bf16[2,2,1,64,512]{4,3,2,1,0:T(8,128)(2,1)S(1)}, u32[]{:S(2)}, u32[]{:S(2)}) collective-permute-start(bf16[2,2,1,64,512]{4,3,2,1,0:T(8,128)(2,1)S(1)} %get-tuple-element.29), channel_id=1, source_target_pairs={{0,1},{1,2},{2,3},{3,4},{4,5},{5,6},{6,7},{7,8},{8,9},{9,10},{10,1... | collective-permute-start | bytes 786440 | tf_op jit(solution)/shard_map/ppermute | solution.py:24
  8.3 9.7 %collective-permute-start.1 = (bf16[2,2,1,64,512]{4,3,2,1,0:T(8,128)(2,1)S(1)}, bf16[2,2,1,64,512]{4,3,2,1,0:T(8,128)(2,1)S(1)}, u32[]{:S(2)}, u32[]{:S(2)}) collective-permute-start(bf16[2,2,1,64,512]{4,3,2,1,0:T(8,128)(2,1)S(1)} %get-tuple-element.30), channel_id=1, source_target_pairs={{1,0},{2,1},{3,2},{4,3},{5,4},{6,5},{7,6},{8,7},{9,8},{10,9},{11,1... | collective-permute-start | bytes 786440 | tf_op jit(solution)/shard_map/ppermute | solution.py:25
  18.2 13.4 %collective-permute-start.2 = (bf16[2,1,4,64,512]{4,3,2,1,0:T(8,128)(2,1)S(1)}, bf16[2,1,4,64,512]{4,3,2,1,0:T(8,128)(2,1)S(1)}, u32[]{:S(2)}, u32[]{:S(2)}) collective-permute-start(bf16[2,1,4,64,512]{4,3,2,1,0:T(8,128)(2,1)S(1)} %get-tuple-element.27), channel_id=1, source_target_pairs={{0,32},{32,64},{64,96},{1,33},{33,65},{65,97},{2,34},{34,66},{66,9... | collective-permute-start | bytes 1572872 | tf_op jit(solution)/shard_map/ppermute | solution.py:24
  21.6 14.1 %collective-permute-start.3 = (bf16[2,1,4,64,512]{4,3,2,1,0:T(8,128)(2,1)S(1)}, bf16[2,1,4,64,512]{4,3,2,1,0:T(8,128)(2,1)S(1)}, u32[]{:S(2)}, u32[]{:S(2)}) collective-permute-start(bf16[2,1,4,64,512]{4,3,2,1,0:T(8,128)(2,1)S(1)} %get-tuple-element.28), channel_id=1, source_target_pairs={{32,0},{64,32},{96,64},{33,1},{65,33},{97,65},{34,2},{66,34},{98,6... | collective-permute-start | bytes 1572872 | tf_op jit(solution)/shard_map/ppermute | solution.py:25
  36.0 19.5 %copy-start.2 = (s32[2,2,2]{2,1,0:T(2,128)S(1)}, s32[2,2,2]{2,1,0:T(2,128)}, u32[]{:S(2)}) copy-start(s32[2,2,2]{2,1,0:T(2,128)} %param.10) | copy-start | bytes 100
  37.1 27.6 %collective-permute-start.4 = (bf16[1,4,4,64,512]{4,3,2,1,0:T(8,128)(2,1)}, bf16[1,4,4,64,512]{4,3,2,1,0:T(8,128)(2,1)}, u32[]{:S(2)}, u32[]{:S(2)}) collective-permute-start(bf16[1,4,4,64,512]{4,3,2,1,0:T(8,128)(2,1)} %get-tuple-element.25), channel_id=1, source_target_pairs={{0,128},{1,129},{2,130},{3,131},{4,132},{5,133},{6,134},{7,135},{8... | collective-permute-start | bytes 3145736 | tf_op jit(solution)/shard_map/ppermute | solution.py:24
  39.4 25.3 %collective-permute-start.5 = (bf16[1,4,4,64,512]{4,3,2,1,0:T(8,128)(2,1)S(1)}, bf16[1,4,4,64,512]{4,3,2,1,0:T(8,128)(2,1)}, u32[]{:S(2)}, u32[]{:S(2)}) collective-permute-start(bf16[1,4,4,64,512]{4,3,2,1,0:T(8,128)(2,1)S(1)} %get-tuple-element.26), channel_id=1, source_target_pairs={{128,0},{129,1},{130,2},{131,3},{132,4},{133,5},{134,6},{135,7},{1... | collective-permute-start | bytes 3145736 | tf_op jit(solution)/shard_map/ppermute | solution.py:25
  41.9 22.0 %all-to-all-start = ((s32[32,1,1]{2,1,0:T(1,128)}), s32[32,1,1]{2,1,0:T(1,128)S(1)}, u32[]{:S(2)}, u32[]{:S(2)}) async-start(s32[32,1,1]{2,1,0:T(1,128)} %broadcast_in_dim.44), calls=%async_computation | async-start | bytes 32768 | tf_op jit(solution)/shard_map/all_to_all | solution.py:152
  80.5 7.3 %collective-permute-start.6 = (bf16[9,3,3,64,192]{4,3,2,1,0:T(8,128)(2,1)}, bf16[9,3,3,64,192]{4,3,2,1,0:T(8,128)(2,1)S(1)}, u32[]{:S(2)}, u32[]{:S(2)}) collective-permute-start(bf16[9,3,3,64,192]{4,3,2,1,0:T(8,128)(2,1)} %bitcast.49), channel_id=1, source_target_pairs={{0,128},{1,129},{2,130},{3,131},{4,132},{5,133},{6,134},{7,135},{8... | collective-permute-start | bytes 5971976 | tf_op jit(solution)/shard_map/ppermute | solution.py:138
  83.2 7.1 %collective-permute-start.7 = (bf16[9,3,3,64,192]{4,3,2,1,0:T(8,128)(2,1)}, bf16[9,3,3,64,192]{4,3,2,1,0:T(8,128)(2,1)S(1)}, u32[]{:S(2)}, u32[]{:S(2)}) collective-permute-start(bf16[9,3,3,64,192]{4,3,2,1,0:T(8,128)(2,1)} %bitcast.48), channel_id=1, source_target_pairs={{128,0},{129,1},{130,2},{131,3},{132,4},{133,5},{134,6},{135,7},{1... | collective-permute-start | bytes 5971976 | tf_op jit(solution)/shard_map/ppermute | solution.py:139
  94.5 36.2 %collective-permute-start.8 = (bf16[3,5,3,64,192]{4,3,2,1,0:T(8,128)(2,1)S(1)}, bf16[3,5,3,64,192]{4,3,2,1,0:T(8,128)(2,1)S(1)}, u32[]{:S(2)}, u32[]{:S(2)}) collective-permute-start(bf16[3,5,3,64,192]{4,3,2,1,0:T(8,128)(2,1)S(1)} %get-tuple-element.21), channel_id=1, source_target_pairs={{0,1},{1,2},{2,3},{3,4},{4,5},{5,6},{6,7},{7,8},{8,9},{9,10},{10,1... | collective-permute-start | bytes 3317768 | tf_op jit(solution)/shard_map/ppermute | solution.py:138
  97.2 35.9 %collective-permute-start.9 = (bf16[3,5,3,64,192]{4,3,2,1,0:T(8,128)(2,1)S(1)}, bf16[3,5,3,64,192]{4,3,2,1,0:T(8,128)(2,1)S(1)}, u32[]{:S(2)}, u32[]{:S(2)}) collective-permute-start(bf16[3,5,3,64,192]{4,3,2,1,0:T(8,128)(2,1)S(1)} %get-tuple-element.22), channel_id=1, source_target_pairs={{1,0},{2,1},{3,2},{4,3},{5,4},{6,5},{7,6},{8,7},{9,8},{10,9},{11,1... | collective-permute-start | bytes 3317768 | tf_op jit(solution)/shard_map/ppermute | solution.py:139
  134.6 18.3 %collective-permute-start.10 = (bf16[5,3,64,320]{3,2,1,0:T(8,128)(2,1)S(1)}, bf16[5,3,64,320]{3,2,1,0:T(8,128)(2,1)S(1)}, u32[]{:S(2)}, u32[]{:S(2)}) collective-permute-start(bf16[5,3,64,320]{3,2,1,0:T(8,128)(2,1)S(1)} %get-tuple-element.23), channel_id=1, source_target_pairs={{0,32},{32,64},{64,96},{1,33},{33,65},{65,97},{2,34},{34,66},{66,9... | collective-permute-start | bytes 1843208 | tf_op jit(solution)/shard_map/ppermute | solution.py:138
  138.0 19.0 %collective-permute-start.11 = (bf16[5,3,64,320]{3,2,1,0:T(8,128)(2,1)S(1)}, bf16[5,3,64,320]{3,2,1,0:T(8,128)(2,1)S(1)}, u32[]{:S(2)}, u32[]{:S(2)}) collective-permute-start(bf16[5,3,64,320]{3,2,1,0:T(8,128)(2,1)S(1)} %get-tuple-element.24), channel_id=1, source_target_pairs={{32,0},{64,32},{96,64},{33,1},{65,33},{97,65},{34,2},{66,34},{98,6... | collective-permute-start | bytes 1843208 | tf_op jit(solution)/shard_map/ppermute | solution.py:139
  160.6 35.0 %all-to-all-start.1 = ((bf16[32,64,256]{2,1,0:T(8,128)(2,1)}), bf16[32,64,256]{2,1,0:T(8,128)(2,1)S(1)}, u32[]{:S(2)}, u32[]{:S(2)}) async-start(bf16[32,64,256]{2,1,0:T(8,128)(2,1)} %bitcast.33), calls=%async_computation.1 | async-start | bytes 2097152 | tf_op jit(solution)/shard_map/all_to_all | solution.py:166
  196.6 55.1 %copy-start.1 = (bf16[2,2,2,64,512]{4,3,2,1,0:T(8,128)(2,1)S(1)}, bf16[2,2,2,64,512]{4,3,2,1,0:T(8,128)(2,1)}, u32[]{:S(2)}) copy-start(bf16[2,2,2,64,512]{4,3,2,1,0:T(8,128)(2,1)} %param.11) | copy-start | bytes 1572868

commit v3 on v2

--- a/solution.py
+++ b/solution.py
@@ -152,11 +152,11 @@
     targets = lax.all_to_all(target, "gz", split_axis=0, concat_axis=0, tiled=True).reshape(group_size)
 
     wide_placed = extend(place_rows(p_blocks, p_cols, p_count))
-    wide_placed, targets = lax.optimization_barrier((wide_placed, targets))
     low, mid, high = contributions(a_blocks, a_cols, a_count, wide_placed, interpret)
     low, mid, high = (x.reshape(9, 3, 3, B, 3 * B) for x in (low, mid, high))
     part = fold(low, mid, high, "gx", 1, 1).reshape(3, 3, 5, 3, B, 3 * B)
     part = fold(part[0], part[1], part[2], "gz", 4, B)
+    part, targets = lax.optimization_barrier((part, targets))
     part = fold(part[0], part[1], part[2], "gy", 1, 1).astype(jnp.bfloat16)
     coarse = part.reshape(25, B, 5 * B).transpose(1, 0, 2).reshape(B, 125 * B)
     coarse = jnp.pad(coarse, ((0, 0), (0, 3 * B)))

time: 252 us -> 250 us (level)
  blocking collectives: 53.5 us -> 92.8 us
  waiting for transfers between devices: 109 us -> 71.7 us
  starting transfers between devices: 51.5 us -> 38.4 us
  local copies, waits for them, and re-layouts: 10.5 us -> 14.6 us
  other arithmetic: 12.3 us -> 16.2 us
    all_to_all x0 -> x1, blocking collectives: none -> 39.1 us  [local(): lax.all_to_all(target, 'gz', split_axis=0, concat_axis=0, tiled=True)]
    ppermute x3, waiting for transfers between devices: 46.5 us -> 16.8 us  [fold(): from_below = lax.ppermute(high.astype(jnp.bfloat16), axis, up)]
    all_to_all x1 -> x0, starting transfers between devices: 13.5 us -> none  [local(): lax.all_to_all(target, 'gz', split_axis=0, concat_axis=0, tiled=True)]
    all_to_all x1 -> x0, waiting for transfers between devices: 7.87 us -> none  [local(): lax.all_to_all(target, 'gz', split_axis=0, concat_axis=0, tiled=True)]
    slice x2, local copies, waits for them, and re-layouts: 0.54 us -> 4 us  [local(): part = fold(part[0], part[1], part[2], 'gz', 4, B)]
    ppermute x3, waiting for transfers between devices: 7.36 us -> 10.1 us  [extend(): after = lax.ppermute(lax.slice_in_dim(shard, 0, 1, axis=dim), axis, down)]
  transfers between devices with their start and end apart: 14 -> 13, of which waited for: 12 -> 10; matrix products, arithmetic and copies ran while one was open for 1% -> 2% of each run, Pallas kernels for 0% -> 0%
where the time goes in v3:
time: 250 us; the launch traced here: 249 us
  blocking collectives  92.8 us (37%)
  waiting for transfers between devices  71.7 us (29%)
  starting transfers between devices  38.4 us (15%)
  other arithmetic  16.2 us (6%)
  local copies, waits for them, and re-layouts  14.6 us (6%)
  Pallas kernels  12.2 us (5%)
    all_to_all x1, blocking collectives, local(): mine = lax.all_to_all(sent, 'gz', split_axis=0, concat_axis=0, tiled=True)  53.7 us
    all_to_all x1, blocking collectives, local(): lax.all_to_all(target, 'gz', split_axis=0, concat_axis=0, tiled=True)  39.1 us
    all_to_all x1, waiting for transfers between devices, local(): lax.all_to_all(spread, 'gz', split_axis=0, concat_axis=0, tiled=True)  25.5 us
    ppermute x3, waiting for transfers between devices, fold(): from_below = lax.ppermute(high.astype(jnp.bfloat16), axis, up)  16.8 us
    ppermute x3, waiting for transfers between devices, extend(): lax.ppermute(lax.slice_in_dim(shard, length - 1, length, axis=dim), axis,...  12.7 us
    pallas_call x1, Pallas kernels, contributions(): pl.pallas_call(galerkin_kernel, out_shape=[jax.ShapeDtypeStruct((9, 9, B,...  12.2 us
    ppermute x3, waiting for transfers between devices, extend(): after = lax.ppermute(lax.slice_in_dim(shard, 0, 1, axis=dim), axis, down)  10.1 us
    all_to_all x1, starting transfers between devices, local(): lax.all_to_all(spread, 'gz', split_axis=0, concat_axis=0, tiled=True)  10.1 us
  transfers between devices with their start and end apart: 13, of which 10 were waited for; matrix products, arithmetic and copies ran while one was open for 2% of the time, Pallas kernels for 0%

profile of v3, /device:TPU:8, one launch (start us, length us, event | category | flops | bytes accessed | tf_op | source)
XLA Modules:
  0.0 248.9 jit_solution(4481407860202472728)
XLA Ops:
  4.8 3.5 %collective-permute-start = (bf16[2,2,1,64,512]{4,3,2,1,0:T(8,128)(2,1)S(1)}, bf16[2,2,1,64,512]{4,3,2,1,0:T(8,128)(2,1)S(1)}, u32[]{:S(2)}, u32[]{:S(2)}) collective-permute-start(bf16[2,2,1,64,512]{4,3,2,1,0:T(8,128)(2,1)S(1)} %get-tuple-element.27), channel_id=1, source_target_pairs={{0,1},{1,2},{2,3},{3,4},{4,5},{5,6},{6,7},{7,8},{8,9},{9,10},{10,1... | collective-permute-start | bytes 786440 | tf_op jit(solution)/shard_map/ppermute | solution.py:24
  8.3 2.4 collective-permute-start.1
  10.7 4.1 %collective-permute-done = bf16[2,2,1,64,512]{4,3,2,1,0:T(8,128)(2,1)S(1)} collective-permute-done((bf16[2,2,1,64,512]{4,3,2,1,0:T(8,128)(2,1)S(1)}, bf16[2,2,1,64,512]{4,3,2,1,0:T(8,128)(2,1)S(1)}, u32[]{:S(2)}, u32[]{:S(2)}) %collective-permute-start) | collective-permute-done | bytes 262176 | tf_op jit(solution)/shard_map/ppermute | solution.py:24
  14.7 3.2 %collective-permute-done.1 = bf16[2,2,1,64,512]{4,3,2,1,0:T(8,128)(2,1)S(1)} collective-permute-done((bf16[2,2,1,64,512]{4,3,2,1,0:T(8,128)(2,1)S(1)}, bf16[2,2,1,64,512]{4,3,2,1,0:T(8,128)(2,1)S(1)}, u32[]{:S(2)}, u32[]{:S(2)}) %collective-permute-start.1) | collective-permute-done | bytes 262176 | tf_op jit(solution)/shard_map/ppermute | solution.py:25
  18.2 3.4 %collective-permute-start.2 = (bf16[2,1,4,64,512]{4,3,2,1,0:T(8,128)(2,1)S(1)}, bf16[2,1,4,64,512]{4,3,2,1,0:T(8,128)(2,1)S(1)}, u32[]{:S(2)}, u32[]{:S(2)}) collective-permute-start(bf16[2,1,4,64,512]{4,3,2,1,0:T(8,128)(2,1)S(1)} %get-tuple-element.25), channel_id=1, source_target_pairs={{0,32},{32,64},{64,96},{1,33},{33,65},{65,97},{2,34},{34,66},{66,9... | collective-permute-start | bytes 1572872 | tf_op jit(solution)/shard_map/ppermute | solution.py:24
  22.9 8.6 %collective-permute-done.2 = bf16[2,1,4,64,512]{4,3,2,1,0:T(8,128)(2,1)S(1)} collective-permute-done((bf16[2,1,4,64,512]{4,3,2,1,0:T(8,128)(2,1)S(1)}, bf16[2,1,4,64,512]{4,3,2,1,0:T(8,128)(2,1)S(1)}, u32[]{:S(2)}, u32[]{:S(2)}) %collective-permute-start.2) | collective-permute-done | bytes 524320 | tf_op jit(solution)/shard_map/ppermute | solution.py:24
  31.5 4.1 %collective-permute-done.3 = bf16[2,1,4,64,512]{4,3,2,1,0:T(8,128)(2,1)S(1)} collective-permute-done((bf16[2,1,4,64,512]{4,3,2,1,0:T(8,128)(2,1)S(1)}, bf16[2,1,4,64,512]{4,3,2,1,0:T(8,128)(2,1)S(1)}, u32[]{:S(2)}, u32[]{:S(2)}) %collective-permute-start.3) | collective-permute-done | bytes 524320 | tf_op jit(solution)/shard_map/ppermute | solution.py:25
  37.1 2.3 collective-permute-start.4
  41.3 2.8 %collective-permute-done.5 = bf16[1,4,4,64,512]{4,3,2,1,0:T(8,128)(2,1)} collective-permute-done((bf16[1,4,4,64,512]{4,3,2,1,0:T(8,128)(2,1)S(1)}, bf16[1,4,4,64,512]{4,3,2,1,0:T(8,128)(2,1)}, u32[]{:S(2)}, u32[]{:S(2)}) %collective-permute-start.5) | collective-permute-done | bytes 1048608 | tf_op jit(solution)/shard_map/ppermute | solution.py:25
  44.1 3.5 %pad_maximum_fusion = bf16[4,4,4,64,512]{4,3,2,1,0:T(8,128)(2,1)} fusion(bf16[1,4,4,64,512]{4,3,2,1,0:T(8,128)(2,1)} %collective-permute-done.5, bf16[2,1,4,64,512]{4,3,2,1,0:T(8,128)(2,1)S(1)} %collective-permute-done.3, bf16[2,2,1,64,512]{4,3,2,1,0:T(8,128)(2,1)S(1)} %collective-permute-done.1, bf16[2,2,2,64,512]{4,3,2,1,0:T(8,128)(2,1)S(1)} %bitcast.41, ...), kind=kLoop, calls=%fused_computation.6 | loop fusion | flops 12582912 | bytes 8388608 | tf_op jit(solution)/shard_map/concatenate | solution.py:26
  47.6 12.2 %shard_map.82 = (bf16[9,9,64,192]{3,2,1,0:T(8,128)(2,1)}, f32[9,9,64,192]{3,2,1,0:T(8,128)}, bf16[9,9,64,192]{3,2,1,0:T(8,128)(2,1)}) custom-call(s32[8,32]{1,0:T(8,128)} %bitcast.47, s32[8]{0:T(128)} %reshape.120.count, bf16[8,64,2048]{2,1,0:T(8,128)(2,1)} %bitcast.45, bf16[64,64,512]{2,1,0:T(8,128)(2,1)} %bitcast.36), custom_call_target="tpu_custom_call" | custom-call | tf_op jit(solution)/shard_map/pallas_call | solution.py:119
  59.7 2.2 collective-permute-start.6
  63.3 3.3 %collective-permute-done.6 = bf16[9,3,3,64,192]{4,3,2,1,0:T(8,128)(2,1)S(1)} collective-permute-done((bf16[9,3,3,64,192]{4,3,2,1,0:T(8,128)(2,1)}, bf16[9,3,3,64,192]{4,3,2,1,0:T(8,128)(2,1)S(1)}, u32[]{:S(2)}, u32[]{:S(2)}) %collective-permute-start.6) | collective-permute-done | bytes 1990688 | tf_op jit(solution)/shard_map/ppermute | solution.py:138
  66.6 2.5 collective-permute-done.7
  69.0 6.2 %fusion.13 = (bf16[9,5,3,64,192]{4,3,2,1,0:T(8,128)(2,1)S(1)}, f32[9,5,3,64,192]{4,3,2,1,0:T(8,128)}) fusion(bf16[9,3,3,64,192]{4,3,2,1,0:T(8,128)(2,1)S(1)} %collective-permute-done.7, f32[9,3,3,64,192]{4,3,2,1,0:T(8,128)} %bitcast.42, bf16[9,3,3,64,192]{4,3,2,1,0:T(8,128)(2,1)S(1)} %collective-permute-done.6), kind=kLoop, calls=%fused_computation.31 | loop fusion | flops 8294400 | bytes 17915904 | tf_op jit(solution)/shard_map/convert.15
  77.1 3.2 %collective-permute-start.8 = (bf16[3,5,3,64,192]{4,3,2,1,0:T(8,128)(2,1)}, bf16[3,5,3,64,192]{4,3,2,1,0:T(8,128)(2,1)S(1)}, u32[]{:S(2)}, u32[]{:S(2)}) collective-permute-start(bf16[3,5,3,64,192]{4,3,2,1,0:T(8,128)(2,1)} %get-tuple-element.19), channel_id=1, source_target_pairs={{0,1},{1,2},{2,3},{3,4},{4,5},{5,6},{6,7},{7,8},{8,9},{9,10},{10,1... | collective-permute-start | bytes 3317768 | tf_op jit(solution)/shard_map/ppermute | solution.py:138
  80.2 2.7 %collective-permute-start.9 = (bf16[3,5,3,64,192]{4,3,2,1,0:T(8,128)(2,1)}, bf16[3,5,3,64,192]{4,3,2,1,0:T(8,128)(2,1)S(1)}, u32[]{:S(2)}, u32[]{:S(2)}) collective-permute-start(bf16[3,5,3,64,192]{4,3,2,1,0:T(8,128)(2,1)} %get-tuple-element.20), channel_id=1, source_target_pairs={{1,0},{2,1},{3,2},{4,3},{5,4},{6,5},{7,6},{8,7},{9,8},{10,9},{11,1... | collective-permute-start | bytes 3317768 | tf_op jit(solution)/shard_map/ppermute | solution.py:139
  83.7 39.1 %all_to_all.16 = s32[32,1,1]{2,1,0:T(1,128)S(1)} all-to-all(s32[32,1,1]{2,1,0:T(1,128)S(1)} %broadcast_in_dim.44), channel_id=1, replica_groups=mesh['gx'=2,'gy'=4,'gz'=32] {'gz'}, dimensions={0} | all-to-all | bytes 256 | tf_op jit(solution)/shard_map/all_to_all | solution.py:152
  127.4 3.4 %collective-permute-start.10 = (bf16[5,3,64,320]{3,2,1,0:T(8,128)(2,1)S(1)}, bf16[5,3,64,320]{3,2,1,0:T(8,128)(2,1)S(1)}, u32[]{:S(2)}, u32[]{:S(2)}) collective-permute-start(bf16[5,3,64,320]{3,2,1,0:T(8,128)(2,1)S(1)} %get-tuple-element.21), channel_id=1, source_target_pairs={{0,32},{32,64},{64,96},{1,33},{33,65},{65,97},{2,34},{34,66},{66,9... | collective-permute-start | bytes 1843208 | tf_op jit(solution)/shard_map/ppermute | solution.py:138
  132.3 13.4 %collective-permute-done.10 = bf16[5,3,64,320]{3,2,1,0:T(8,128)(2,1)S(1)} collective-permute-done((bf16[5,3,64,320]{3,2,1,0:T(8,128)(2,1)S(1)}, bf16[5,3,64,320]{3,2,1,0:T(8,128)(2,1)S(1)}, u32[]{:S(2)}, u32[]{:S(2)}) %collective-permute-start.10) | collective-permute-done | bytes 614432 | tf_op jit(solution)/shard_map/ppermute | solution.py:138
  145.7 4.2 %collective-permute-done.11 = bf16[5,3,64,320]{3,2,1,0:T(8,128)(2,1)S(1)} collective-permute-done((bf16[5,3,64,320]{3,2,1,0:T(8,128)(2,1)S(1)}, bf16[5,3,64,320]{3,2,1,0:T(8,128)(2,1)S(1)}, u32[]{:S(2)}, u32[]{:S(2)}) %collective-permute-start.11) | collective-permute-done | bytes 614432 | tf_op jit(solution)/shard_map/ppermute | solution.py:139
  153.5 10.1 %all-to-all-start.1 = ((bf16[32,64,256]{2,1,0:T(8,128)(2,1)}), bf16[32,64,256]{2,1,0:T(8,128)(2,1)S(1)}, u32[]{:S(2)}, u32[]{:S(2)}) async-start(bf16[32,64,256]{2,1,0:T(8,128)(2,1)} %bitcast.33), calls=%async_computation.1 | async-start | bytes 2097152 | tf_op jit(solution)/shard_map/all_to_all | solution.py:166
  164.3 25.5 %all-to-all-done.1 = bf16[32,64,256]{2,1,0:T(8,128)(2,1)S(1)} async-done(((bf16[32,64,256]{2,1,0:T(8,128)(2,1)}), bf16[32,64,256]{2,1,0:T(8,128)(2,1)S(1)}, u32[]{:S(2)}, u32[]{:S(2)}) %all-to-all-start.1) | async-done | bytes 1048608 | tf_op jit(solution)/shard_map/all_to_all | solution.py:166
  193.6 53.7 %all_to_all.17 = bf16[64,64,256]{2,1,0:T(8,128)(2,1)S(1)} all-to-all(bf16[64,64,256]{2,1,0:T(8,128)(2,1)S(1)} %broadcast_select_fusion), channel_id=1, replica_groups=mesh['gx'=2,'gy'=4,'gz'=32] {'gz'}, dimensions={0} | all-to-all | bytes 4194304 | tf_op jit(solution)/shard_map/all_to_all | solution.py:174
  (48 shorter events, 28.3 us)
Async XLA Ops:
  0.0 2.7 %copy-start = (bf16[2,2,2,64,512]{4,3,2,1,0:T(8,128)(2,1)S(1)}, bf16[2,2,2,64,512]{4,3,2,1,0:T(8,128)(2,1)}, u32[]{:S(2)}) copy-start(bf16[2,2,2,64,512]{4,3,2,1,0:T(8,128)(2,1)} %param.11) | copy-start | bytes 1572868
  4.8 9.9 %collective-permute-start = (bf16[2,2,1,64,512]{4,3,2,1,0:T(8,128)(2,1)S(1)}, bf16[2,2,1,64,512]{4,3,2,1,0:T(8,128)(2,1)S(1)}, u32[]{:S(2)}, u32[]{:S(2)}) collective-permute-start(bf16[2,2,1,64,512]{4,3,2,1,0:T(8,128)(2,1)S(1)} %get-tuple-element.27), channel_id=1, source_target_pairs={{0,1},{1,2},{2,3},{3,4},{4,5},{5,6},{6,7},{7,8},{8,9},{9,10},{10,1... | collective-permute-start | bytes 786440 | tf_op jit(solution)/shard_map/ppermute | solution.py:24
  8.3 9.7 %collective-permute-start.1 = (bf16[2,2,1,64,512]{4,3,2,1,0:T(8,128)(2,1)S(1)}, bf16[2,2,1,64,512]{4,3,2,1,0:T(8,128)(2,1)S(1)}, u32[]{:S(2)}, u32[]{:S(2)}) collective-permute-start(bf16[2,2,1,64,512]{4,3,2,1,0:T(8,128)(2,1)S(1)} %get-tuple-element.28), channel_id=1, source_target_pairs={{1,0},{2,1},{3,2},{4,3},{5,4},{6,5},{7,6},{8,7},{9,8},{10,9},{11,1... | collective-permute-start | bytes 786440 | tf_op jit(solution)/shard_map/ppermute | solution.py:25
  18.2 13.4 %collective-permute-start.2 = (bf16[2,1,4,64,512]{4,3,2,1,0:T(8,128)(2,1)S(1)}, bf16[2,1,4,64,512]{4,3,2,1,0:T(8,128)(2,1)S(1)}, u32[]{:S(2)}, u32[]{:S(2)}) collective-permute-start(bf16[2,1,4,64,512]{4,3,2,1,0:T(8,128)(2,1)S(1)} %get-tuple-element.25), channel_id=1, source_target_pairs={{0,32},{32,64},{64,96},{1,33},{33,65},{65,97},{2,34},{34,66},{66,9... | collective-permute-start | bytes 1572872 | tf_op jit(solution)/shard_map/ppermute | solution.py:24
  21.6 14.1 %collective-permute-start.3 = (bf16[2,1,4,64,512]{4,3,2,1,0:T(8,128)(2,1)S(1)}, bf16[2,1,4,64,512]{4,3,2,1,0:T(8,128)(2,1)S(1)}, u32[]{:S(2)}, u32[]{:S(2)}) collective-permute-start(bf16[2,1,4,64,512]{4,3,2,1,0:T(8,128)(2,1)S(1)} %get-tuple-element.26), channel_id=1, source_target_pairs={{32,0},{64,32},{96,64},{33,1},{65,33},{97,65},{34,2},{66,34},{98,6... | collective-permute-start | bytes 1572872 | tf_op jit(solution)/shard_map/ppermute | solution.py:25
  36.0 4.7 %copy-start.2 = (s32[2,2,2]{2,1,0:T(2,128)S(1)}, s32[2,2,2]{2,1,0:T(2,128)}, u32[]{:S(2)}) copy-start(s32[2,2,2]{2,1,0:T(2,128)} %param.10) | copy-start | bytes 100
  37.1 4.2 %collective-permute-start.4 = (bf16[1,4,4,64,512]{4,3,2,1,0:T(8,128)(2,1)}, bf16[1,4,4,64,512]{4,3,2,1,0:T(8,128)(2,1)}, u32[]{:S(2)}, u32[]{:S(2)}) collective-permute-start(bf16[1,4,4,64,512]{4,3,2,1,0:T(8,128)(2,1)} %get-tuple-element.23), channel_id=1, source_target_pairs={{0,128},{1,129},{2,130},{3,131},{4,132},{5,133},{6,134},{7,135},{8... | collective-permute-start | bytes 3145736 | tf_op jit(solution)/shard_map/ppermute | solution.py:24
  39.4 4.7 %collective-permute-start.5 = (bf16[1,4,4,64,512]{4,3,2,1,0:T(8,128)(2,1)S(1)}, bf16[1,4,4,64,512]{4,3,2,1,0:T(8,128)(2,1)}, u32[]{:S(2)}, u32[]{:S(2)}) collective-permute-start(bf16[1,4,4,64,512]{4,3,2,1,0:T(8,128)(2,1)S(1)} %get-tuple-element.24), channel_id=1, source_target_pairs={{128,0},{129,1},{130,2},{131,3},{132,4},{133,5},{134,6},{135,7},{1... | collective-permute-start | bytes 3145736 | tf_op jit(solution)/shard_map/ppermute | solution.py:25
  59.7 6.8 %collective-permute-start.6 = (bf16[9,3,3,64,192]{4,3,2,1,0:T(8,128)(2,1)}, bf16[9,3,3,64,192]{4,3,2,1,0:T(8,128)(2,1)S(1)}, u32[]{:S(2)}, u32[]{:S(2)}) collective-permute-start(bf16[9,3,3,64,192]{4,3,2,1,0:T(8,128)(2,1)} %bitcast.49), channel_id=1, source_target_pairs={{0,128},{1,129},{2,130},{3,131},{4,132},{5,133},{6,134},{7,135},{8... | collective-permute-start | bytes 5971976 | tf_op jit(solution)/shard_map/ppermute | solution.py:138
  62.0 7.1 %collective-permute-start.7 = (bf16[9,3,3,64,192]{4,3,2,1,0:T(8,128)(2,1)}, bf16[9,3,3,64,192]{4,3,2,1,0:T(8,128)(2,1)S(1)}, u32[]{:S(2)}, u32[]{:S(2)}) collective-permute-start(bf16[9,3,3,64,192]{4,3,2,1,0:T(8,128)(2,1)} %bitcast.48), channel_id=1, source_target_pairs={{128,0},{129,1},{130,2},{131,3},{132,4},{133,5},{134,6},{135,7},{1... | collective-permute-start | bytes 5971976 | tf_op jit(solution)/shard_map/ppermute | solution.py:139
  77.1 48.6 %collective-permute-start.8 = (bf16[3,5,3,64,192]{4,3,2,1,0:T(8,128)(2,1)}, bf16[3,5,3,64,192]{4,3,2,1,0:T(8,128)(2,1)S(1)}, u32[]{:S(2)}, u32[]{:S(2)}) collective-permute-start(bf16[3,5,3,64,192]{4,3,2,1,0:T(8,128)(2,1)} %get-tuple-element.19), channel_id=1, source_target_pairs={{0,1},{1,2},{2,3},{3,4},{4,5},{5,6},{6,7},{7,8},{8,9},{9,10},{10,1... | collective-permute-start | bytes 3317768 | tf_op jit(solution)/shard_map/ppermute | solution.py:138
  80.2 45.4 %collective-permute-start.9 = (bf16[3,5,3,64,192]{4,3,2,1,0:T(8,128)(2,1)}, bf16[3,5,3,64,192]{4,3,2,1,0:T(8,128)(2,1)S(1)}, u32[]{:S(2)}, u32[]{:S(2)}) collective-permute-start(bf16[3,5,3,64,192]{4,3,2,1,0:T(8,128)(2,1)} %get-tuple-element.20), channel_id=1, source_target_pairs={{1,0},{2,1},{3,2},{4,3},{5,4},{6,5},{7,6},{8,7},{9,8},{10,9},{11,1... | collective-permute-start | bytes 3317768 | tf_op jit(solution)/shard_map/ppermute | solution.py:139
  127.4 18.3 %collective-permute-start.10 = (bf16[5,3,64,320]{3,2,1,0:T(8,128)(2,1)S(1)}, bf16[5,3,64,320]{3,2,1,0:T(8,128)(2,1)S(1)}, u32[]{:S(2)}, u32[]{:S(2)}) collective-permute-start(bf16[5,3,64,320]{3,2,1,0:T(8,128)(2,1)S(1)} %get-tuple-element.21), channel_id=1, source_target_pairs={{0,32},{32,64},{64,96},{1,33},{33,65},{65,97},{2,34},{34,66},{66,9... | collective-permute-start | bytes 1843208 | tf_op jit(solution)/shard_map/ppermute | solution.py:138
  130.9 19.0 %collective-permute-start.11 = (bf16[5,3,64,320]{3,2,1,0:T(8,128)(2,1)S(1)}, bf16[5,3,64,320]{3,2,1,0:T(8,128)(2,1)S(1)}, u32[]{:S(2)}, u32[]{:S(2)}) collective-permute-start(bf16[5,3,64,320]{3,2,1,0:T(8,128)(2,1)S(1)} %get-tuple-element.22), channel_id=1, source_target_pairs={{32,0},{64,32},{96,64},{33,1},{65,33},{97,65},{34,2},{66,34},{98,6... | collective-permute-start | bytes 1843208 | tf_op jit(solution)/shard_map/ppermute | solution.py:139
  153.5 36.3 %all-to-all-start.1 = ((bf16[32,64,256]{2,1,0:T(8,128)(2,1)}), bf16[32,64,256]{2,1,0:T(8,128)(2,1)S(1)}, u32[]{:S(2)}, u32[]{:S(2)}) async-start(bf16[32,64,256]{2,1,0:T(8,128)(2,1)} %bitcast.33), calls=%async_computation.1 | async-start | bytes 2097152 | tf_op jit(solution)/shard_map/all_to_all | solution.py:166
  193.6 55.3 %copy-start.1 = (bf16[2,2,2,64,512]{4,3,2,1,0:T(8,128)(2,1)S(1)}, bf16[2,2,2,64,512]{4,3,2,1,0:T(8,128)(2,1)}, u32[]{:S(2)}) copy-start(bf16[2,2,2,64,512]{4,3,2,1,0:T(8,128)(2,1)} %param.11) | copy-start | bytes 1572868
